TPU v7x, 256 devices: a whole 4x4x8 slice. The times are simulated.
256 devices in a mesh: lon: 16 (over x_lo, y, core), rep: 16 (over z, x_hi).
Axes of the slice: x: 4 (x_hi: 2, x_lo: 2; x = x_hi * 2 + x_lo), y: 4, z: 8, core: 2. Of those that a mesh axis runs over, the one named last changes fastest.
Arguments:
- fields: bfloat16 [256, 24, 128, 256], P('rep', None, 'lon'), may hold values from -6 to 6
- stem_weight: bfloat16 [32, 24, 4, 4], replicated, may hold values from -0.3125 to 0.3125
- mid_weight: bfloat16 [64, 32, 3, 3], replicated, may hold values from -0.375 to 0.375
- head_weight: bfloat16 [64, 64, 3, 3], replicated, may hold values from -0.25 to 0.25
- out_weight: float32 [64], replicated, may hold values from -0.75 to 0.75
- pred_cotangent: float32 [256, 32, 64], P(('rep', 'lon')), may hold values from -6 to 6
Outputs:
- prediction: float32 [256, 32, 64], P(('rep', 'lon'))
- stem_cotangent: bfloat16 [256, 32, 64, 128], P('rep', None, 'lon')
- grad_stem: float32 [32, 24, 4, 4], replicated
- grad_mid: float32 [64, 32, 3, 3], replicated
- grad_head: float32 [64, 64, 3, 3], replicated
- grad_out: float32 [64], replicated
All inputs are finite; a program needn't handle non-finite values.
Results may differ from a plain program's by a relative error of at most 0.0085.
Values may be sent and summed in bfloat16 or wider, within the bound.
No kernel may reach another device: no remote copies, remote signals or barrier semaphores. Data moves between devices by JAX's collectives and lax.ppermute only.
A program may use at most 128 MiB of HBM per device.

v0:
```python
import jax
import jax.numpy as jnp
from jax import lax
from jax.experimental import pallas as pl
from jax.experimental.pallas import tpu as pltpu
from jax.sharding import PartitionSpec as P

BF16, F32 = jnp.bfloat16, jnp.float32
SLABS, CIN, SLAB_LON, LAT = 16, 24, 8, 256
C1, C2 = 32, 64
STEM_GROUP, MID_GROUP, HEAD_GROUP = 4, 2, 2


def one_hot(shape, test):
    rows = lax.broadcasted_iota(jnp.int32, shape, 0)
    cols = lax.broadcasted_iota(jnp.int32, shape, 1)
    return jnp.where(test(rows, cols), 1.0, 0.0).astype(BF16)


def selections():
    regroup = one_hot(
        (CIN * SLAB_LON, CIN * SLAB_LON),
        lambda r, c: (r % CIN == c // SLAB_LON) & (r // CIN == c % SLAB_LON),
    )
    field_taps = one_hot((LAT, 512), lambda r, c: r == 2 * (c % 128) + c // 128 - 1)
    stem_taps = one_hot(
        (256, 384),
        lambda r, c: (r // 128 == c % 128 // 64) & (r % 128 == 2 * (c % 64) + c // 128 - 1),
    )
    interleave = one_hot(
        (256, 256),
        lambda r, c: (r % 128 // 64 == c // 128) & (c % 128 == 2 * (r % 64) + r // 128),
    )
    slab_rows = one_hot((128, 128), lambda r, c: (r % 4 == c // C1) & (r // 4 == c % C1))
    return regroup, field_taps, stem_taps, interleave, slab_rows


def toeplitz(rows, group, step):
    out, window, depth = rows.shape
    width = step * (group - 1) + window
    copies = [
        jnp.pad(rows, ((0, 0), (step * at, width - window - step * at), (0, 0))) for at in range(group)
    ]
    return jnp.stack(copies).reshape(group * out, width * depth)


def kernel_weights(stem_weight, mid_weight, head_weight):
    stem = stem_weight.transpose(0, 2, 3, 1).reshape(C1, 4, 4 * CIN)
    mid = mid_weight.transpose(0, 2, 3, 1).reshape(C2, 3, 3 * C1)
    head = head_weight.transpose(0, 2, 3, 1).reshape(C2, 3, 3 * C2)
    head_back = head_weight[:, :, ::-1, ::-1].transpose(1, 2, 3, 0).reshape(C2, 3, 3 * C2)
    none = jnp.zeros((C1, C2), mid_weight.dtype)
    blocks = []
    for lat_odd in (0, 1):
        for lon_odd in (0, 1):
            row = []
            for next_lon in (0, 1):
                for next_lat in (0, 1):
                    if next_lon > lon_odd or next_lat > lat_odd:
                        row.append(none)
                    else:
                        a = 1 if not lon_odd else 2 - 2 * next_lon
                        b = 1 if not lat_odd else 2 - 2 * next_lat
                        row.append(mid_weight[:, :, a, b].T)
            blocks.append(jnp.concatenate(row, 1))
    mid_back = jnp.concatenate(blocks, 0)
    return (
        toeplitz(stem, STEM_GROUP, 2),
        toeplitz(mid, MID_GROUP, 2),
        toeplitz(head, HEAD_GROUP, 1),
        toeplitz(head_back, HEAD_GROUP, 1),
        mid_back,
    )


def dot(left, right):
    return jnp.dot(left, right, preferred_element_type=F32)


def dot_t(left, right):
    return lax.dot_general(left, right, (((1,), (1,)), ((), ())), preferred_element_type=F32)


def swapped(block):
    return pltpu.roll(block.astype(F32), 64, 1).astype(BF16)


def sigmoid(values):
    return 1.0 / (1.0 + jnp.exp(-values))


def slope_of(values):
    sigma = sigmoid(values)
    return sigma * (1.0 + values * (1.0 - sigma))


def scenario_kernel(
    x_ref, w1_ref, w2_ref, w3_ref, w3b_ref, w2b_ref, regroup_ref, ftaps_ref, staps_ref, inter_ref, rows_ref,
    ow_ref, pc_ref,
    pred_ref, cot_ref, sums_ref,
    fx, stem_pre, mx, mid_pre, hx, hc_wide, hc_pad, mc_pair, mc_pad, sc_pad,
):
    lane = lax.broadcasted_iota(jnp.int32, (C2, 128), 1) % 64
    first, last = lane == 0, lane == 63

    def earlier(block):
        return jnp.where(first, 0.0, pltpu.roll(block, 1, 1))

    def later(block):
        return jnp.where(last, 0.0, pltpu.roll(block, 127, 1))

    def load_slab(s, _):
        for half in (0, 1):
            part = dot(regroup_ref[...], x_ref[s + 8 * half]).astype(BF16)
            taps = dot(part, ftaps_ref[...])
            wide = jnp.concatenate(
                [taps[:, 128 * b : 128 * b + 128].reshape(SLAB_LON, CIN, 128) for b in range(4)], 1
            )
            fx[pl.ds(1 + s * SLAB_LON, SLAB_LON), :, half * 128 : half * 128 + 128] = wide.astype(BF16)
        return 0

    lax.fori_loop(0, 8, load_slab, 0)
    fx[0, :, 0:128] = fx[64, :, 128:256]
    fx[0, :, 128:256] = fx[64, :, 0:128]
    fx[65, :, 0:128] = fx[1, :, 128:256]
    fx[65, :, 128:256] = fx[1, :, 0:128]

    def stem(g, _):
        n = STEM_GROUP
        window = fx[pl.ds(2 * n * g, 2 * n + 2)].reshape((2 * n + 2) * 96, 256)
        pre = dot(w1_ref[...], window)
        stem_pre[pl.ds(n * g, n)] = pre.reshape(n, C1, 256)
        act = (pre * sigmoid(pre)).astype(BF16)
        taps = dot(act, staps_ref[...])
        wide = jnp.concatenate([taps[:, 128 * b : 128 * b + 128].reshape(n, C1, 128) for b in range(3)], 1)
        mx[pl.ds(1 + n * g, n)] = wide.astype(BF16)
        return 0

    lax.fori_loop(0, 32 // STEM_GROUP, stem, 0)
    mx[0] = swapped(mx[32])
    mx[33] = jnp.zeros((96, 128), BF16)

    def mid(g, _):
        n = MID_GROUP
        window = mx[pl.ds(2 * n * g, 2 * n + 1)].reshape((2 * n + 1) * 96, 128)
        pre = dot(w2_ref[...], window)
        mid_pre[pl.ds(n * g, n)] = pre.reshape(n, C2, 128)
        act = pre * sigmoid(pre)
        for k in range(n):
            one = act[k * C2 : k * C2 + C2]
            hx[n * g + k + 1] = jnp.concatenate([earlier(one), one, later(one)], 0).astype(BF16)
        return 0

    lax.fori_loop(0, 16 // MID_GROUP, mid, 0)
    hx[0] = swapped(hx[16])
    hx[17] = swapped(hx[1])

    for edge in (0, 1, 18, 19):
        hc_pad[edge] = jnp.zeros((C2, 128), BF16)
    out_w = jnp.broadcast_to(ow_ref[...], (C2, 128))

    def head(g, out_sum):
        n = HEAD_GROUP
        window = hx[pl.ds(n * g, n + 2)].reshape((n + 2) * 192, 128)
        pre = dot(w3_ref[...], window)
        sigma = sigmoid(pre)
        act = (pre * sigma).astype(BF16).astype(F32)
        bend = sigma * (1.0 + pre * (1.0 - sigma))
        for k in range(n):
            r = n * g + k
            here = slice(k * C2, k * C2 + C2)
            cot = jnp.broadcast_to(pc_ref[pl.ds(r, 1), :], (C2, 128))
            pred_ref[pl.ds(r, 1), :] = jnp.sum(out_w * act[here], 0, keepdims=True)
            out_sum = out_sum + cot * act[here]
            hc = (cot * out_w) * bend[here]
            hc_pad[r + 2] = hc.astype(BF16)
            hc_wide[r + 1] = jnp.concatenate([earlier(hc), hc, later(hc)], 0).astype(BF16)
        return out_sum

    out_sum = lax.fori_loop(0, 16 // HEAD_GROUP, head, jnp.zeros((C2, 128), F32))
    sums_ref[576:640, :] = out_sum
    hc_wide[0] = swapped(hc_wide[16])
    hc_wide[17] = swapped(hc_wide[1])

    for edge in (0, 17):
        mc_pad[edge] = jnp.zeros((C2, 128), BF16)

    def head_back(g, _):
        n = HEAD_GROUP
        window = hc_wide[pl.ds(n * g, n + 2)].reshape((n + 2) * 192, 128)
        grad = dot(w3b_ref[...], window).astype(BF16).astype(F32)
        mc = grad * slope_of(mid_pre[pl.ds(n * g, n)].reshape(n * C2, 128))
        for k in range(n):
            one = mc[k * C2 : k * C2 + C2]
            mc_pad[n * g + k + 1] = one.astype(BF16)
            mc_pair[n * g + k] = jnp.concatenate([one, later(one)], 0).astype(BF16)
        return 0

    lax.fori_loop(0, 16 // HEAD_GROUP, head_back, 0)
    mc_pair[16] = swapped(mc_pair[0])

    for edge in (0, 33):
        sc_pad[edge] = jnp.zeros((C1, 256), BF16)

    def mid_back(m, _):
        parts = []
        for k in range(2):
            window = mc_pair[pl.ds(2 * m + k, 2)].reshape(256, 128)
            grad = dot(w2b_ref[...], window).astype(BF16)
            parts.append(jnp.concatenate([grad[0:64], grad[64:128]], 1))
        grad = dot(jnp.concatenate(parts, 0), inter_ref[...])
        cot = (grad * slope_of(stem_pre[pl.ds(4 * m, 4)].reshape(128, 256))).astype(BF16)
        sc_pad[pl.ds(4 * m + 1, 4)] = cot.reshape(4, C1, 256)
        out = dot(rows_ref[...], cot).astype(BF16)
        cot_ref[m] = out[:, 0:128]
        cot_ref[m + 8] = out[:, 128:256]
        return 0

    lax.fori_loop(0, 8, mid_back, 0)

    def head_sum(p, total):
        left = jnp.concatenate([hc_pad[pl.ds(2 * p + k, 3)].reshape(192, 128) for k in range(2)], 1)
        right = jnp.concatenate([hx[2 * p], hx[2 * p + 1]], 1)
        return total + dot_t(left, right)

    total = lax.fori_loop(0, 9, head_sum, jnp.zeros((192, 192), F32))
    sums_ref[0:192, :] = total[:, 0:128]
    sums_ref[192:384, 0:64] = total[:, 128:192]

    def mid_sum(m, total):
        return total + dot_t(mx[pl.ds(2 * m, 2)].reshape(192, 128), mc_pad[pl.ds(m, 2)].reshape(128, 128))

    sums_ref[384:576, :] = lax.fori_loop(0, 17, mid_sum, jnp.zeros((192, 128), F32))

    def stem_sum(m, total):
        return total + dot_t(fx[pl.ds(2 * m, 2)].reshape(192, 256), sc_pad[pl.ds(m, 2)].reshape(64, 256))

    sums_ref[192:384, 64:128] = lax.fori_loop(0, 33, stem_sum, jnp.zeros((192, 64), F32))


def scenario_pass(x, weights, out_weight, cotangent):
    out_shape = (
        jax.ShapeDtypeStruct((16, 128), F32),
        jax.ShapeDtypeStruct((SLABS, 128, 128), BF16),
        jax.ShapeDtypeStruct((640, 128), F32),
    )
    scratch = [
        pltpu.VMEM((66, 96, 256), BF16),
        pltpu.VMEM((32, C1, 256), F32),
        pltpu.VMEM((34, 96, 128), BF16),
        pltpu.VMEM((16, C2, 128), F32),
        pltpu.VMEM((18, 192, 128), BF16),
        pltpu.VMEM((18, 192, 128), BF16),
        pltpu.VMEM((20, C2, 128), BF16),
        pltpu.VMEM((17, 128, 128), BF16),
        pltpu.VMEM((18, C2, 128), BF16),
        pltpu.VMEM((34, C1, 256), BF16),
    ]
    whole = pl.BlockSpec(memory_space=pltpu.VMEM)
    return pl.pallas_call(
        scenario_kernel,
        out_shape=out_shape,
        in_specs=[whole] * 13,
        out_specs=(whole,) * 3,
        scratch_shapes=scratch,
        compiler_params=pltpu.CompilerParams(vmem_limit_bytes=48 << 20),
        cost_estimate=pl.CostEstimate(flops=4 * 10**9, bytes_accessed=4 << 20, transcendentals=10**6),
        name="scenario",
    )(x, *weights, *selections(), out_weight.reshape(C2, 1), cotangent)


def exchanged(value, axis):
    return lax.all_to_all(value, axis, split_axis=0, concat_axis=0, tiled=True)


def summed_everywhere(terms):
    lon, rep = lax.axis_size("lon"), lax.axis_size("rep")
    shape = (terms.shape[0] // lon, 128)
    share = exchanged(terms.reshape(lon, *shape), "lon").sum(0)
    share = exchanged(jnp.broadcast_to(share[None], (rep, *shape)), "rep").sum(0)
    return exchanged(jnp.broadcast_to(share[None], (lon, *shape)), "lon").reshape(terms.shape)


def unpacked(sums):
    head = jnp.concatenate([sums[0:192], sums[192:384, 0:64]], 1)
    head = head.reshape(3, C2, 3, C2)[::-1].transpose(1, 3, 0, 2)
    mid = sums[384:576].reshape(2, 3, C1, 2, C2)
    mid = jnp.stack([mid[0, :, :, 1], mid[1, :, :, 1], mid[0, :, :, 0]])
    stem = sums[192:384, 64:128].reshape(2, 4, CIN, 2, C1)
    stem = jnp.stack([stem[0, :, :, 1], stem[1, :, :, 1], stem[0, :, :, 0], stem[1, :, :, 0]])
    return stem.transpose(3, 2, 0, 1), mid.transpose(3, 2, 0, 1), head, sums[576:640].sum(1)


def local(fields, stem_weight, mid_weight, head_weight, out_weight, pred_cotangent):
    x = exchanged(fields.reshape(SLABS, CIN * SLAB_LON, LAT), "lon")
    weights = kernel_weights(stem_weight, mid_weight, head_weight)
    cotangent = pred_cotangent.reshape(2, 16, 64).transpose(1, 0, 2).reshape(16, 128)
    prediction, stem_cotangent, sums = scenario_pass(x, weights, out_weight, cotangent)
    prediction = prediction.reshape(16, 2, 64).transpose(1, 0, 2).reshape(1, 32, 64)
    stem_cotangent = exchanged(stem_cotangent, "lon").reshape(SLABS, C1, 4, 128)
    grads = unpacked(summed_everywhere(sums))
    factor = 1.0 / (fields.shape[0] * lax.axis_size("rep"))
    return (prediction, stem_cotangent, *(grad * factor for grad in grads))


def solution(mesh):
    placed = (P("rep", None, "lon", None), P(), P(), P(), P(), P(("rep", "lon"), None, None))
    return jax.shard_map(
        local,
        mesh=mesh,
        in_specs=placed,
        out_specs=(P(("rep", "lon"), None, None), P("rep", None, "lon", None), P(), P(), P(), P()),
        check_vma=False,
    )
```

profile of v0, /device:TPU:1, one launch (start us, length us, event | category | flops | bytes accessed | tf_op | source)
XLA Modules:
  0.0 128.1 jit_solution(14018103488733885101)
XLA Ops:
  0.7 7.1 %all-to-all-start = ((bf16[16,192,256]{2,1,0:T(8,128)(2,1)}), bf16[16,192,256]{2,1,0:T(8,128)(2,1)S(1)}, u32[]{:S(2)}, u32[]{:S(2)}) async-start(bf16[16,192,256]{2,1,0:T(8,128)(2,1)} %bitcast.106), calls=%async_computation | async-start | bytes 3145728 | tf_op jit(solution)/shard_map/all_to_all | solution.py:273
  8.1 0.1 reshape.85.pc_ref
  8.1 0.1 copy.90.ow_ref
  8.2 0.2 copy.79
  8.4 0.1 reshape.75
  8.6 0.1 copy.84
  8.7 0.2 copy.86
  8.9 0.1 pad_bitcast_fusion.3
  9.0 0.2 pad_maximum_fusion.2
  9.3 0.2 reshape.82.w3b_ref
  9.6 0.1 pad_maximum_fusion
  9.7 0.2 copy.85
  9.9 0.2 reshape.80.w3_ref
  10.3 0.2 copy.100
  10.5 0.2 reshape.94.w2_ref
  10.7 0.1 pad_maximum_fusion.1
  10.8 0.2 copy.80
  11.0 0.4 reshape.76.w1_ref
  11.4 0.1 fusion.20.w2b_ref
  11.5 0.2 select_convert_fusion.4.rows_ref
  11.7 0.2 select_convert_fusion.3.regroup_ref
  11.9 0.6 select_convert_fusion.2.inter_ref
  12.5 0.3 select_convert_fusion.1.staps_ref
  12.7 0.1 select_convert_fusion.ftaps_ref
  12.8 16.7 %all-to-all-done.x_ref = bf16[16,192,256]{2,1,0:T(8,128)(2,1)S(1)} async-done(((bf16[16,192,256]{2,1,0:T(8,128)(2,1)}), bf16[16,192,256]{2,1,0:T(8,128)(2,1)S(1)}, u32[]{:S(2)}, u32[]{:S(2)}) %all-to-all-start) | async-done | bytes 1572896 | tf_op jit(solution)/shard_map/all_to_all | solution.py:273
  29.5 29.2 %scenario.1 = (f32[16,128]{1,0:T(8,128)S(1)}, bf16[16,128,128]{2,1,0:T(8,128)(2,1)}, f32[640,128]{1,0:T(8,128)S(1)}) custom-call(bf16[16,192,256]{2,1,0:T(8,128)(2,1)S(1)} %all-to-all-done.x_ref, bf16[128,960]{1,0:T(8,128)(2,1)S(1)} %reshape.76.w1_ref, bf16[128,480]{1,0:T(8,128)(2,1)S(1)} %reshape.94.w2_ref, bf16[128,768]{1,0:T(8,128)(2,1)S(1)} %reshape.80.w3_ref, ...), custom_call_target="tpu_custom_call" | custom-call | flops 4000000000 | bytes 4194304 | tf_op jit(solution)/shard_map/scenario/pallas_call | solution.py:260
  58.7 12.3 %all_to_all.25 = f32[16,40,128]{2,1,0:T(8,128)S(1)} all-to-all(f32[16,40,128]{2,1,0:T(8,128)S(1)} %bitcast.101), channel_id=1, replica_groups=mesh['lon'=16,'rep'=16] {'lon'}, dimensions={0} | all-to-all | bytes 655360 | tf_op jit(solution)/shard_map/all_to_all | solution.py:273
  71.1 22.7 %all_to_all.26 = f32[16,40,128]{2,1,0:T(8,128)S(1)} all-to-all(f32[16,40,128]{2,1,0:T(8,128)S(1)} %broadcast_in_dim.66), channel_id=1, replica_groups=mesh['lon'=16,'rep'=16] {'rep'}, dimensions={0} | all-to-all | bytes 655360 | tf_op jit(solution)/shard_map/all_to_all | solution.py:273
  93.8 6.8 %all-to-all-start.1 = ((bf16[16,128,128]{2,1,0:T(8,128)(2,1)}), bf16[16,128,128]{2,1,0:T(8,128)(2,1)S(1)}, u32[]{:S(2)}, u32[]{:S(2)}) async-start(bf16[16,128,128]{2,1,0:T(8,128)(2,1)} %get-tuple-element.10), calls=%async_computation.1 | async-start | bytes 1048576 | tf_op jit(solution)/shard_map/all_to_all | solution.py:273
  100.6 9.9 %all-to-all-done.1 = bf16[16,128,128]{2,1,0:T(8,128)(2,1)S(1)} async-done(((bf16[16,128,128]{2,1,0:T(8,128)(2,1)}), bf16[16,128,128]{2,1,0:T(8,128)(2,1)S(1)}, u32[]{:S(2)}, u32[]{:S(2)}) %all-to-all-start.1) | async-done | bytes 524320 | tf_op jit(solution)/shard_map/all_to_all | solution.py:273
  110.4 0.7 broadcast_in_dim.67
  111.2 4.5 %all-to-all-start.4 = ((f32[16,40,128]{2,1,0:T(8,128)}), f32[16,40,128]{2,1,0:T(8,128)S(1)}, u32[]{:S(2)}, u32[]{:S(2)}) async-start(f32[16,40,128]{2,1,0:T(8,128)} %broadcast_in_dim.67), calls=%async_computation.4 | async-start | bytes 655360 | tf_op jit(solution)/shard_map/all_to_all | solution.py:273
  115.7 0.1 reshape.86
  115.8 0.6 copy.91
  116.4 7.1 %all-to-all-done.4 = f32[16,40,128]{2,1,0:T(8,128)S(1)} async-done(((f32[16,40,128]{2,1,0:T(8,128)}), f32[16,40,128]{2,1,0:T(8,128)S(1)}, u32[]{:S(2)}, u32[]{:S(2)}) %all-to-all-start.4) | async-done | bytes 327712 | tf_op jit(solution)/shard_map/all_to_all | solution.py:273
  123.5 0.1 slice_reduce_fusion
  123.6 0.1 fusion.49
  123.7 0.5 broadcast_multiply_fusion
  124.2 0.2 reshape.93
  124.4 0.1 multiply_bitcast_fusion
  124.5 0.7 copy.98
  125.2 0.2 reshape.92
  125.4 0.1 fusion.50
  125.5 0.2 reshape.91
  125.7 0.2 fusion.51
  125.9 0.7 copy.97
  126.6 0.7 fusion.16
  127.3 0.8 copy.110
  (50 shorter events, 0.5 us)
Async XLA Ops:
  0.6 7.4 %copy-start.3 = (f32[1,32,64]{2,1,0:T(8,128)S(1)}, f32[1,32,64]{2,1,0:T(8,128)}, u32[]{:S(2)}) copy-start(f32[1,32,64]{2,1,0:T(8,128)} %param.11) | copy-start | bytes 24580
  0.6 7.5 %copy-start.4 = (f32[64]{0:T(128)S(1)}, f32[64]{0:T(128)}, u32[]{:S(2)}) copy-start(f32[64]{0:T(128)} %param.10) | copy-start | bytes 772
  0.7 7.6 %copy-start.2 = (bf16[32,24,4,4]{0,3,2,1:T(4,128)(2,1)S(1)}, bf16[32,24,4,4]{0,3,2,1:T(4,128)(2,1)}, u32[]{:S(2)}) copy-start(bf16[32,24,4,4]{0,3,2,1:T(4,128)(2,1)} %param.7) | copy-start | bytes 73732
  0.7 7.9 %copy-start = (bf16[64,64,3,3]{1,0,3,2:T(8,128)(2,1)S(1)}, bf16[64,64,3,3]{1,0,3,2:T(8,128)(2,1)}, u32[]{:S(2)}) copy-start(bf16[64,64,3,3]{1,0,3,2:T(8,128)(2,1)} %param.9) | copy-start | bytes 221188
  0.7 28.9 %all-to-all-start = ((bf16[16,192,256]{2,1,0:T(8,128)(2,1)}), bf16[16,192,256]{2,1,0:T(8,128)(2,1)S(1)}, u32[]{:S(2)}, u32[]{:S(2)}) async-start(bf16[16,192,256]{2,1,0:T(8,128)(2,1)} %bitcast.106), calls=%async_computation | async-start | bytes 3145728 | tf_op jit(solution)/shard_map/all_to_all | solution.py:273
  9.3 0.9 copy-start.1
  93.8 16.7 %all-to-all-start.1 = ((bf16[16,128,128]{2,1,0:T(8,128)(2,1)}), bf16[16,128,128]{2,1,0:T(8,128)(2,1)S(1)}, u32[]{:S(2)}, u32[]{:S(2)}) async-start(bf16[16,128,128]{2,1,0:T(8,128)(2,1)} %get-tuple-element.10), calls=%async_computation.1 | async-start | bytes 1048576 | tf_op jit(solution)/shard_map/all_to_all | solution.py:273
  111.2 12.3 %all-to-all-start.4 = ((f32[16,40,128]{2,1,0:T(8,128)}), f32[16,40,128]{2,1,0:T(8,128)S(1)}, u32[]{:S(2)}, u32[]{:S(2)}) async-start(f32[16,40,128]{2,1,0:T(8,128)} %broadcast_in_dim.67), calls=%async_computation.4 | async-start | bytes 655360 | tf_op jit(solution)/shard_map/all_to_all | solution.py:273
where the time goes:
time: 129 us; the launch traced here: 128 us
  blocking collectives  35 us (27%)
  waiting for transfers between devices  33.6 us (26%)
  Pallas kernels  29.2 us (23%)
  starting transfers between devices  18.3 us (14%)
  local copies, waits for them, and re-layouts  7.32 us (6%)
  other arithmetic  3.46 us (3%)
    all_to_all x2, blocking collectives, exchanged(): return lax.all_to_all(value, axis, split_axis=0, concat_axis=0, tiled=True)  35 us
    all_to_all x3, waiting for transfers between devices, exchanged(): return lax.all_to_all(value, axis, split_axis=0, concat_axis=0, tiled=True)  33.6 us
    pallas_call x1, Pallas kernels, scenario_pass(): pl.pallas_call(scenario_kernel, out_shape=out_shape, in_specs=[whole] * 1...  29.2 us
    all_to_all x3, starting transfers between devices, exchanged(): return lax.all_to_all(value, axis, split_axis=0, concat_axis=0, tiled=True)  18.3 us
  transfers between devices with their start and end apart: 3, of which 3 were waited for; matrix products, arithmetic and copies ran while one was open for 4% of the time, Pallas kernels for 0%

commit v1 on v0

--- a/solution.py
+++ b/solution.py
@@ -1,3 +1,5 @@
+import functools
+
 import jax
 import jax.numpy as jnp
 from jax import lax
@@ -8,6 +10,8 @@
 BF16, F32 = jnp.bfloat16, jnp.float32
 SLABS, CIN, SLAB_LON, LAT = 16, 24, 8, 256
 C1, C2 = 32, 64
+COT_ROWS, SHARE = 128, 40
+WIRE_ROWS = COT_ROWS + 2 * SHARE
 STEM_GROUP, MID_GROUP, HEAD_GROUP = 4, 2, 2
 
 
@@ -97,8 +101,8 @@
 def scenario_kernel(
     x_ref, w1_ref, w2_ref, w3_ref, w3b_ref, w2b_ref, regroup_ref, ftaps_ref, staps_ref, inter_ref, rows_ref,
     ow_ref, pc_ref,
-    pred_ref, cot_ref, sums_ref,
-    fx, stem_pre, mx, mid_pre, hx, hc_wide, hc_pad, mc_pair, mc_pad, sc_pad,
+    pred_ref, wire_ref,
+    sums_ref, fx, stem_pre, mx, mid_pre, hx, hc_wide, hc_pad, mc_pair, mc_pad, sc_pad,
 ):
     lane = lax.broadcasted_iota(jnp.int32, (C2, 128), 1) % 64
     first, last = lane == 0, lane == 63
@@ -212,8 +216,8 @@
         cot = (grad * slope_of(stem_pre[pl.ds(4 * m, 4)].reshape(128, 256))).astype(BF16)
         sc_pad[pl.ds(4 * m + 1, 4)] = cot.reshape(4, C1, 256)
         out = dot(rows_ref[...], cot).astype(BF16)
-        cot_ref[m] = out[:, 0:128]
-        cot_ref[m + 8] = out[:, 128:256]
+        wire_ref[m, 0:COT_ROWS] = out[:, 0:128]
+        wire_ref[m + 8, 0:COT_ROWS] = out[:, 128:256]
         return 0
 
     lax.fori_loop(0, 8, mid_back, 0)
@@ -237,14 +241,19 @@
 
     sums_ref[192:384, 64:128] = lax.fori_loop(0, 33, stem_sum, jnp.zeros((192, 64), F32))
 
+    for s in range(SLABS):
+        term = sums_ref[s * SHARE : s * SHARE + SHARE, :]
+        near = term.astype(BF16).astype(F32)
+        wire_ref[s, COT_ROWS:WIRE_ROWS] = jnp.concatenate([near, term - near], 0).astype(BF16)
+
 
 def scenario_pass(x, weights, out_weight, cotangent):
     out_shape = (
         jax.ShapeDtypeStruct((16, 128), F32),
-        jax.ShapeDtypeStruct((SLABS, 128, 128), BF16),
-        jax.ShapeDtypeStruct((640, 128), F32),
+        jax.ShapeDtypeStruct((SLABS, WIRE_ROWS, 128), BF16),
     )
     scratch = [
+        pltpu.VMEM((SLABS * SHARE, 128), F32),
         pltpu.VMEM((66, 96, 256), BF16),
         pltpu.VMEM((32, C1, 256), F32),
         pltpu.VMEM((34, 96, 128), BF16),
@@ -261,7 +270,7 @@
         scenario_kernel,
         out_shape=out_shape,
         in_specs=[whole] * 13,
-        out_specs=(whole,) * 3,
+        out_specs=(whole,) * 2,
         scratch_shapes=scratch,
         compiler_params=pltpu.CompilerParams(vmem_limit_bytes=48 << 20),
         cost_estimate=pl.CostEstimate(flops=4 * 10**9, bytes_accessed=4 << 20, transcendentals=10**6),
@@ -273,34 +282,83 @@
     return lax.all_to_all(value, axis, split_axis=0, concat_axis=0, tiled=True)
 
 
-def summed_everywhere(terms):
-    lon, rep = lax.axis_size("lon"), lax.axis_size("rep")
-    shape = (terms.shape[0] // lon, 128)
-    share = exchanged(terms.reshape(lon, *shape), "lon").sum(0)
-    share = exchanged(jnp.broadcast_to(share[None], (rep, *shape)), "rep").sum(0)
-    return exchanged(jnp.broadcast_to(share[None], (lon, *shape)), "lon").reshape(terms.shape)
-
-
-def unpacked(sums):
-    head = jnp.concatenate([sums[0:192], sums[192:384, 0:64]], 1)
-    head = head.reshape(3, C2, 3, C2)[::-1].transpose(1, 3, 0, 2)
-    mid = sums[384:576].reshape(2, 3, C1, 2, C2)
-    mid = jnp.stack([mid[0, :, :, 1], mid[1, :, :, 1], mid[0, :, :, 0]])
-    stem = sums[192:384, 64:128].reshape(2, 4, CIN, 2, C1)
-    stem = jnp.stack([stem[0, :, :, 1], stem[1, :, :, 1], stem[0, :, :, 0], stem[1, :, :, 0]])
-    return stem.transpose(3, 2, 0, 1), mid.transpose(3, 2, 0, 1), head, sums[576:640].sum(1)
+def lon_share_kernel(got_ref, out_ref):
+    total = jnp.zeros((2 * SHARE, 128), F32)
+    for k in range(SLABS):
+        total = total + got_ref[k, COT_ROWS:WIRE_ROWS].astype(F32)
+    share = (total[0:SHARE] + total[SHARE : 2 * SHARE]).astype(BF16)
+    for k in range(SLABS):
+        out_ref[k] = share
+
+
+def rep_share_kernel(got_ref, out_ref):
+    total = jnp.zeros((SHARE, 128), F32)
+    for k in range(SLABS):
+        total = total + got_ref[k].astype(F32)
+    share = total.astype(BF16)
+    for k in range(SLABS):
+        out_ref[k] = share
+
+
+def unpack_kernel(factor, sums_ref, stem_ref, mid_ref, head_ref, out_ref, wide):
+    wide[...] = sums_ref[...].astype(F32) * factor
+    for a in range(3):
+        at = (2 - a) * C2
+        head_ref[a, 0] = wide[at : at + C2, 0:64]
+        head_ref[a, 1] = wide[at : at + C2, 64:128]
+        head_ref[a, 2] = wide[192 + at : 192 + at + C2, 0:64]
+        lanes = slice(0, 64) if a == 2 else slice(64, 128)
+        for b in range(3):
+            at = 384 + a % 2 * 96 + b * C1
+            mid_ref[a, b] = wide[at : at + C1, lanes]
+    for a in range(4):
+        lanes = slice(64, 96) if a >= 2 else slice(96, 128)
+        for c in range(CIN):
+            rows = wide[pl.ds(192 + a % 2 * 96 + c, 4, stride=CIN), :]
+            stem_ref[c, a] = rows[:, lanes]
+    ones = jnp.full((8, 128), 1.0, BF16)
+    out_ref[...] = dot_t(ones, sums_ref[576:640])[0:1] * factor
+
+
+def on_chip(kernel, outs, scratch=(), name=None):
+    whole = pl.BlockSpec(memory_space=pltpu.VMEM)
+    single = not isinstance(outs, tuple)
+    return lambda *args: pl.pallas_call(
+        kernel,
+        out_shape=outs,
+        in_specs=[whole] * len(args),
+        out_specs=whole if single else (whole,) * len(outs),
+        scratch_shapes=scratch,
+        name=name,
+    )(*args)
+
+
+def summed_everywhere(got, factor):
+    shares = jax.ShapeDtypeStruct((SLABS, SHARE, 128), BF16)
+    share = on_chip(lon_share_kernel, shares, name="lon_share")(got)
+    share = on_chip(rep_share_kernel, shares, name="rep_share")(exchanged(share, "rep"))
+    sums = exchanged(share, "lon").reshape(SLABS * SHARE, 128)
+    outs = (
+        jax.ShapeDtypeStruct((CIN, 4, 4, C1), F32),
+        jax.ShapeDtypeStruct((3, 3, C1, C2), F32),
+        jax.ShapeDtypeStruct((3, 3, C2, C2), F32),
+        jax.ShapeDtypeStruct((1, C2), F32),
+    )
+    scratch = [pltpu.VMEM((SLABS * SHARE, 128), F32)]
+    stem, mid, head, out = on_chip(functools.partial(unpack_kernel, factor), outs, scratch, "unpack")(sums)
+    return stem.transpose(3, 0, 1, 2), mid.transpose(3, 2, 0, 1), head.transpose(2, 3, 0, 1), out.reshape(C2)
 
 
 def local(fields, stem_weight, mid_weight, head_weight, out_weight, pred_cotangent):
     x = exchanged(fields.reshape(SLABS, CIN * SLAB_LON, LAT), "lon")
     weights = kernel_weights(stem_weight, mid_weight, head_weight)
     cotangent = pred_cotangent.reshape(2, 16, 64).transpose(1, 0, 2).reshape(16, 128)
-    prediction, stem_cotangent, sums = scenario_pass(x, weights, out_weight, cotangent)
+    prediction, wire = scenario_pass(x, weights, out_weight, cotangent)
     prediction = prediction.reshape(16, 2, 64).transpose(1, 0, 2).reshape(1, 32, 64)
-    stem_cotangent = exchanged(stem_cotangent, "lon").reshape(SLABS, C1, 4, 128)
-    grads = unpacked(summed_everywhere(sums))
+    got = exchanged(wire, "lon")
+    stem_cotangent = got[:, 0:COT_ROWS].reshape(SLABS, C1, 4, 128)
     factor = 1.0 / (fields.shape[0] * lax.axis_size("rep"))
-    return (prediction, stem_cotangent, *(grad * factor for grad in grads))
+    return (prediction, stem_cotangent, *summed_everywhere(got, factor))
 
 
 def solution(mesh):

time: 129 us -> 116 us (0.90)
  waiting for transfers between devices: 33.6 us -> 21.7 us
  starting transfers between devices: 18.3 us -> 12.8 us
  Pallas kernels: 29.2 us -> 34.1 us
  blocking collectives: 35 us -> 39 us
  local copies, waits for them, and re-layouts: 7.32 us -> 4.93 us
  other arithmetic: 3.46 us -> 1.98 us
    all_to_all x3 -> x2, waiting for transfers between devices: 33.6 us -> 21.7 us  [exchanged(): return lax.all_to_all(value, axis, split_axis=0, concat_axis=0, tiled=True)]
    all_to_all x3 -> x2, starting transfers between devices: 18.3 us -> 12.8 us  [exchanged(): return lax.all_to_all(value, axis, split_axis=0, concat_axis=0, tiled=True)]
    pallas_call x0 -> x3, Pallas kernels: none -> 5.43 us  [on_chip(): pl.pallas_call(kernel, out_shape=outs, in_specs=[whole] * len(args), out_...]
    all_to_all x2, blocking collectives: 35 us -> 39 us  [exchanged(): return lax.all_to_all(value, axis, split_axis=0, concat_axis=0, tiled=True)]
    unnamed x13 -> x14, local copies, waits for them, and re-layouts: 2.28 us -> 0.68 us
    mul x4 -> x0, other arithmetic: 1.31 us -> none  [local(): return (prediction, stem_cotangent, *(grad * factor for grad in grads))]
  transfers between devices with their start and end apart: 3 -> 2, of which waited for: 3 -> 2; matrix products, arithmetic and copies ran while one was open for 4% -> 5% of each run, Pallas kernels for 0% -> 0%
where the time goes in v1:
time: 116 us
  blocking collectives  39 us (34%)
  Pallas kernels  34.1 us (29%)
  waiting for transfers between devices  21.7 us (19%)
  starting transfers between devices  12.8 us (11%)
  local copies, waits for them, and re-layouts  4.93 us (4%)
  other arithmetic  1.98 us (2%)
    all_to_all x2, blocking collectives, exchanged(): return lax.all_to_all(value, axis, split_axis=0, concat_axis=0, tiled=True)  39 us
    pallas_call x1, Pallas kernels, scenario_pass(): pl.pallas_call(scenario_kernel, out_shape=out_shape, in_specs=[whole] * 1...  28.7 us
    all_to_all x2, waiting for transfers between devices, exchanged(): return lax.all_to_all(value, axis, split_axis=0, concat_axis=0, tiled=True)  21.7 us
    all_to_all x2, starting transfers between devices, exchanged(): return lax.all_to_all(value, axis, split_axis=0, concat_axis=0, tiled=True)  12.8 us
    pallas_call x3, Pallas kernels, on_chip(): pl.pallas_call(kernel, out_shape=outs, in_specs=[whole] * len(args), out_...  5.43 us
  transfers between devices with their start and end apart: 2, of which 2 were waited for; matrix products, arithmetic and copies ran while one was open for 5% of the time, Pallas kernels for 0%

profile of v1, /device:TPU:1, one launch (start us, length us, event | category | flops | bytes accessed | tf_op | source)
XLA Modules:
  0.0 115.6 jit_solution(10103911004213568244)
XLA Ops:
  0.6 0.0 copy-start.5
  0.6 0.0 copy-start.6
  0.7 0.0 copy-start.4
  0.7 0.0 copy-start.2
  0.7 7.1 %all-to-all-start = ((bf16[16,192,256]{2,1,0:T(8,128)(2,1)}), bf16[16,192,256]{2,1,0:T(8,128)(2,1)S(1)}, u32[]{:S(2)}, u32[]{:S(2)}) async-start(bf16[16,192,256]{2,1,0:T(8,128)(2,1)} %bitcast.81), calls=%async_computation | async-start | bytes 3145728 | tf_op jit(solution)/shard_map/all_to_all | solution.py:282
  8.0 0.0 copy-done.5
  8.1 0.1 reshape.74.pc_ref
  8.1 0.0 copy-done.6
  8.1 0.1 copy.53.ow_ref
  8.2 0.0 copy-done.4
  8.2 0.2 copy.42
  8.4 0.1 reshape.64
  8.6 0.1 copy.47
  8.7 0.2 copy.49
  8.9 0.1 pad_bitcast_fusion.3
  9.0 0.2 pad_maximum_fusion.2
  9.3 0.0 copy-start.3
  9.3 0.2 reshape.71.w3b_ref
  9.5 0.1 pad_bitcast_fusion.1
  9.6 0.1 pad_maximum_fusion
  9.7 0.2 copy.48
  9.9 0.2 reshape.69.w3_ref
  10.2 0.1 pad_maximum_fusion.3
  10.3 0.2 copy.56
  10.5 0.2 reshape.80.w2_ref
  10.7 0.1 pad_maximum_fusion.1
  10.8 0.2 copy.43
  11.0 0.4 reshape.65.w1_ref
  11.4 0.1 fusion.18.w2b_ref
  11.5 0.2 select_convert_fusion.4.rows_ref
  11.7 0.2 select_convert_fusion.3.regroup_ref
  11.9 0.6 select_convert_fusion.2.inter_ref
  12.5 0.3 select_convert_fusion.1.staps_ref
  12.7 0.1 select_convert_fusion.ftaps_ref
  12.8 16.7 %all-to-all-done.x_ref = bf16[16,192,256]{2,1,0:T(8,128)(2,1)S(1)} async-done(((bf16[16,192,256]{2,1,0:T(8,128)(2,1)}), bf16[16,192,256]{2,1,0:T(8,128)(2,1)S(1)}, u32[]{:S(2)}, u32[]{:S(2)}) %all-to-all-start) | async-done | bytes 1572896 | tf_op jit(solution)/shard_map/all_to_all | solution.py:282
  29.5 28.7 %scenario.1 = (f32[16,128]{1,0:T(8,128)S(1)}, bf16[16,208,128]{2,1,0:T(8,128)(2,1)S(1)}) custom-call(bf16[16,192,256]{2,1,0:T(8,128)(2,1)S(1)} %all-to-all-done.x_ref, bf16[128,960]{1,0:T(8,128)(2,1)S(1)} %reshape.65.w1_ref, bf16[128,480]{1,0:T(8,128)(2,1)S(1)} %reshape.80.w2_ref, bf16[128,768]{1,0:T(8,128)(2,1)S(1)} %reshape.69.w3_ref, ...), custom_call_target="tpu_custom_call" | custom-call | flops 4000000000 | bytes 4194304 | tf_op jit(solution)/shard_map/scenario/pallas_call | solution.py:269
  58.2 18.0 %all_to_all.20.got_ref = bf16[16,208,128]{2,1,0:T(8,128)(2,1)} all-to-all(bf16[16,208,128]{2,1,0:T(8,128)(2,1)S(1)} %get-tuple-element.13), channel_id=1, replica_groups=mesh['lon'=16,'rep'=16] {'lon'}, dimensions={0} | all-to-all | bytes 1703936 | tf_op jit(solution)/shard_map/all_to_all | solution.py:282
  76.3 2.0 %lon_share.1 = bf16[16,40,128]{2,1,0:T(8,128)(2,1)} custom-call(bf16[16,208,128]{2,1,0:T(8,128)(2,1)} %all_to_all.20.got_ref), custom_call_target="tpu_custom_call" | custom-call | tf_op jit(solution)/shard_map/lon_share/pallas_call | solution.py:326
  78.2 20.9 %all_to_all.21.got_ref = bf16[16,40,128]{2,1,0:T(8,128)(2,1)} all-to-all(bf16[16,40,128]{2,1,0:T(8,128)(2,1)} %lon_share.1), channel_id=1, replica_groups=mesh['lon'=16,'rep'=16] {'rep'}, dimensions={0} | all-to-all | bytes 327680 | tf_op jit(solution)/shard_map/all_to_all | solution.py:282
  99.2 1.6 %rep_share.1 = bf16[16,40,128]{2,1,0:T(8,128)(2,1)} custom-call(bf16[16,40,128]{2,1,0:T(8,128)(2,1)} %all_to_all.21.got_ref), custom_call_target="tpu_custom_call" | custom-call | tf_op jit(solution)/shard_map/rep_share/pallas_call | solution.py:326
  100.8 5.8 %all-to-all-start.3 = ((bf16[16,40,128]{2,1,0:T(8,128)(2,1)}), bf16[16,40,128]{2,1,0:T(8,128)(2,1)S(1)}, u32[]{:S(2)}, u32[]{:S(2)}) async-start(bf16[16,40,128]{2,1,0:T(8,128)(2,1)} %rep_share.1), calls=%async_computation.3 | async-start | bytes 327680 | tf_op jit(solution)/shard_map/all_to_all | solution.py:282
  106.6 0.1 reshape.75
  106.6 0.6 copy.54
  107.2 0.0 copy-done
  107.3 0.8 slice.40
  108.1 5.0 %all-to-all-done.3 = bf16[16,40,128]{2,1,0:T(8,128)(2,1)S(1)} async-done(((bf16[16,40,128]{2,1,0:T(8,128)(2,1)}), bf16[16,40,128]{2,1,0:T(8,128)(2,1)S(1)}, u32[]{:S(2)}, u32[]{:S(2)}) %all-to-all-start.3) | async-done | bytes 163872 | tf_op jit(solution)/shard_map/all_to_all | solution.py:282
  113.1 0.7 copy-done.1
  113.7 1.9 %unpack.1 = (f32[24,4,4,32]{3,2,1,0:T(4,128)}, f32[3,3,32,64]{3,2,1,0:T(8,128)}, f32[3,3,64,64]{3,2,1,0:T(8,128)}, f32[1,64]{1,0:T(1,128)}) custom-call(bf16[640,128]{1,0:T(8,128)(2,1)} %bitcast.82), custom_call_target="tpu_custom_call" | custom-call | tf_op jit(solution)/shard_map/unpack/pallas_call | solution.py:326
  (36 shorter events, 0.3 us)
Async XLA Ops:
  0.6 7.4 %copy-start.5 = (f32[1,32,64]{2,1,0:T(8,128)S(1)}, f32[1,32,64]{2,1,0:T(8,128)}, u32[]{:S(2)}) copy-start(f32[1,32,64]{2,1,0:T(8,128)} %param.11) | copy-start | bytes 24580
  0.6 7.5 %copy-start.6 = (f32[64]{0:T(128)S(1)}, f32[64]{0:T(128)}, u32[]{:S(2)}) copy-start(f32[64]{0:T(128)} %param.10) | copy-start | bytes 772
  0.7 7.6 %copy-start.4 = (bf16[32,24,4,4]{0,3,2,1:T(4,128)(2,1)S(1)}, bf16[32,24,4,4]{0,3,2,1:T(4,128)(2,1)}, u32[]{:S(2)}) copy-start(bf16[32,24,4,4]{0,3,2,1:T(4,128)(2,1)} %param.7) | copy-start | bytes 73732
  0.7 7.9 %copy-start.2 = (bf16[64,64,3,3]{1,0,3,2:T(8,128)(2,1)S(1)}, bf16[64,64,3,3]{1,0,3,2:T(8,128)(2,1)}, u32[]{:S(2)}) copy-start(bf16[64,64,3,3]{1,0,3,2:T(8,128)(2,1)} %param.9) | copy-start | bytes 221188
  0.7 28.9 %all-to-all-start = ((bf16[16,192,256]{2,1,0:T(8,128)(2,1)}), bf16[16,192,256]{2,1,0:T(8,128)(2,1)S(1)}, u32[]{:S(2)}, u32[]{:S(2)}) async-start(bf16[16,192,256]{2,1,0:T(8,128)(2,1)} %bitcast.81), calls=%async_computation | async-start | bytes 3145728 | tf_op jit(solution)/shard_map/all_to_all | solution.py:282
  9.3 0.9 copy-start.3
  76.3 31.0 %copy-start = (bf16[16,208,128]{2,1,0:T(8,128)(2,1)S(1)}, bf16[16,208,128]{2,1,0:T(8,128)(2,1)}, u32[]{:S(2)}) copy-start(bf16[16,208,128]{2,1,0:T(8,128)(2,1)} %all_to_all.20.got_ref) | copy-start | bytes 2555908
  100.8 12.3 %all-to-all-start.3 = ((bf16[16,40,128]{2,1,0:T(8,128)(2,1)}), bf16[16,40,128]{2,1,0:T(8,128)(2,1)S(1)}, u32[]{:S(2)}, u32[]{:S(2)}) async-start(bf16[16,40,128]{2,1,0:T(8,128)(2,1)} %rep_share.1), calls=%async_computation.3 | async-start | bytes 327680 | tf_op jit(solution)/shard_map/all_to_all | solution.py:282
  113.1 0.7 copy-start.1

commit v2 on v1

--- a/solution.py
+++ b/solution.py
@@ -11,7 +11,8 @@
 SLABS, CIN, SLAB_LON, LAT = 16, 24, 8, 256
 C1, C2 = 32, 64
 COT_ROWS, SHARE = 128, 40
-WIRE_ROWS = COT_ROWS + 2 * SHARE
+SUM_ROWS = 2 * SHARE
+WIRE_ROWS = SUM_ROWS + COT_ROWS
 STEM_GROUP, MID_GROUP, HEAD_GROUP = 4, 2, 2
 
 
@@ -113,49 +114,49 @@
     def later(block):
         return jnp.where(last, 0.0, pltpu.roll(block, 127, 1))
 
-    def load_slab(s, _):
+    def load_slab(s):
         for half in (0, 1):
             part = dot(regroup_ref[...], x_ref[s + 8 * half]).astype(BF16)
             taps = dot(part, ftaps_ref[...])
             wide = jnp.concatenate(
                 [taps[:, 128 * b : 128 * b + 128].reshape(SLAB_LON, CIN, 128) for b in range(4)], 1
             )
-            fx[pl.ds(1 + s * SLAB_LON, SLAB_LON), :, half * 128 : half * 128 + 128] = wide.astype(BF16)
-        return 0
-
-    lax.fori_loop(0, 8, load_slab, 0)
+            fx[1 + s * SLAB_LON : 1 + s * SLAB_LON + SLAB_LON, :, half * 128 : half * 128 + 128] = wide.astype(BF16)
+
+    for step in range(8):
+        load_slab(step)
     fx[0, :, 0:128] = fx[64, :, 128:256]
     fx[0, :, 128:256] = fx[64, :, 0:128]
     fx[65, :, 0:128] = fx[1, :, 128:256]
     fx[65, :, 128:256] = fx[1, :, 0:128]
 
-    def stem(g, _):
+    def stem(g):
         n = STEM_GROUP
         window = fx[pl.ds(2 * n * g, 2 * n + 2)].reshape((2 * n + 2) * 96, 256)
         pre = dot(w1_ref[...], window)
-        stem_pre[pl.ds(n * g, n)] = pre.reshape(n, C1, 256)
+        stem_pre[n * g : n * g + n] = pre.reshape(n, C1, 256)
         act = (pre * sigmoid(pre)).astype(BF16)
         taps = dot(act, staps_ref[...])
         wide = jnp.concatenate([taps[:, 128 * b : 128 * b + 128].reshape(n, C1, 128) for b in range(3)], 1)
-        mx[pl.ds(1 + n * g, n)] = wide.astype(BF16)
-        return 0
-
-    lax.fori_loop(0, 32 // STEM_GROUP, stem, 0)
+        mx[1 + n * g : 1 + n * g + n] = wide.astype(BF16)
+
+    for step in range(32 // STEM_GROUP):
+        stem(step)
     mx[0] = swapped(mx[32])
     mx[33] = jnp.zeros((96, 128), BF16)
 
-    def mid(g, _):
+    def mid(g):
         n = MID_GROUP
         window = mx[pl.ds(2 * n * g, 2 * n + 1)].reshape((2 * n + 1) * 96, 128)
         pre = dot(w2_ref[...], window)
-        mid_pre[pl.ds(n * g, n)] = pre.reshape(n, C2, 128)
+        mid_pre[n * g : n * g + n] = pre.reshape(n, C2, 128)
         act = pre * sigmoid(pre)
         for k in range(n):
             one = act[k * C2 : k * C2 + C2]
             hx[n * g + k + 1] = jnp.concatenate([earlier(one), one, later(one)], 0).astype(BF16)
-        return 0
-
-    lax.fori_loop(0, 16 // MID_GROUP, mid, 0)
+
+    for step in range(16 // MID_GROUP):
+        mid(step)
     hx[0] = swapped(hx[16])
     hx[17] = swapped(hx[1])
 
@@ -173,15 +174,17 @@
         for k in range(n):
             r = n * g + k
             here = slice(k * C2, k * C2 + C2)
-            cot = jnp.broadcast_to(pc_ref[pl.ds(r, 1), :], (C2, 128))
-            pred_ref[pl.ds(r, 1), :] = jnp.sum(out_w * act[here], 0, keepdims=True)
+            cot = jnp.broadcast_to(pc_ref[r : r + 1, :], (C2, 128))
+            pred_ref[r : r + 1, :] = jnp.sum(out_w * act[here], 0, keepdims=True)
             out_sum = out_sum + cot * act[here]
             hc = (cot * out_w) * bend[here]
             hc_pad[r + 2] = hc.astype(BF16)
             hc_wide[r + 1] = jnp.concatenate([earlier(hc), hc, later(hc)], 0).astype(BF16)
         return out_sum
 
-    out_sum = lax.fori_loop(0, 16 // HEAD_GROUP, head, jnp.zeros((C2, 128), F32))
+    out_sum = jnp.zeros((C2, 128), F32)
+    for step in range(16 // HEAD_GROUP):
+        out_sum = head(step, out_sum)
     sums_ref[576:640, :] = out_sum
     hc_wide[0] = swapped(hc_wide[16])
     hc_wide[17] = swapped(hc_wide[1])
@@ -189,62 +192,70 @@
     for edge in (0, 17):
         mc_pad[edge] = jnp.zeros((C2, 128), BF16)
 
-    def head_back(g, _):
+    def head_back(g):
         n = HEAD_GROUP
         window = hc_wide[pl.ds(n * g, n + 2)].reshape((n + 2) * 192, 128)
         grad = dot(w3b_ref[...], window).astype(BF16).astype(F32)
-        mc = grad * slope_of(mid_pre[pl.ds(n * g, n)].reshape(n * C2, 128))
+        mc = grad * slope_of(mid_pre[n * g : n * g + n].reshape(n * C2, 128))
         for k in range(n):
             one = mc[k * C2 : k * C2 + C2]
             mc_pad[n * g + k + 1] = one.astype(BF16)
             mc_pair[n * g + k] = jnp.concatenate([one, later(one)], 0).astype(BF16)
-        return 0
-
-    lax.fori_loop(0, 16 // HEAD_GROUP, head_back, 0)
+
+    for step in range(16 // HEAD_GROUP):
+        head_back(step)
     mc_pair[16] = swapped(mc_pair[0])
 
     for edge in (0, 33):
         sc_pad[edge] = jnp.zeros((C1, 256), BF16)
 
-    def mid_back(m, _):
+    def mid_back(m):
         parts = []
         for k in range(2):
-            window = mc_pair[pl.ds(2 * m + k, 2)].reshape(256, 128)
+            window = mc_pair[2 * m + k : 2 * m + k + 2].reshape(256, 128)
             grad = dot(w2b_ref[...], window).astype(BF16)
             parts.append(jnp.concatenate([grad[0:64], grad[64:128]], 1))
         grad = dot(jnp.concatenate(parts, 0), inter_ref[...])
-        cot = (grad * slope_of(stem_pre[pl.ds(4 * m, 4)].reshape(128, 256))).astype(BF16)
-        sc_pad[pl.ds(4 * m + 1, 4)] = cot.reshape(4, C1, 256)
+        cot = (grad * slope_of(stem_pre[4 * m : 4 * m + 4].reshape(128, 256))).astype(BF16)
+        sc_pad[4 * m + 1 : 4 * m + 1 + 4] = cot.reshape(4, C1, 256)
         out = dot(rows_ref[...], cot).astype(BF16)
-        wire_ref[m, 0:COT_ROWS] = out[:, 0:128]
-        wire_ref[m + 8, 0:COT_ROWS] = out[:, 128:256]
-        return 0
-
-    lax.fori_loop(0, 8, mid_back, 0)
+        wire_ref[m, SUM_ROWS:WIRE_ROWS] = out[:, 0:128]
+        wire_ref[m + 8, SUM_ROWS:WIRE_ROWS] = out[:, 128:256]
+
+    for step in range(8):
+        mid_back(step)
 
     def head_sum(p, total):
-        left = jnp.concatenate([hc_pad[pl.ds(2 * p + k, 3)].reshape(192, 128) for k in range(2)], 1)
+        left = jnp.concatenate([hc_pad[2 * p + k : 2 * p + k + 3].reshape(192, 128) for k in range(2)], 1)
         right = jnp.concatenate([hx[2 * p], hx[2 * p + 1]], 1)
         return total + dot_t(left, right)
 
-    total = lax.fori_loop(0, 9, head_sum, jnp.zeros((192, 192), F32))
+    total = jnp.zeros((192, 192), F32)
+    for step in range(9):
+        total = head_sum(step, total)
     sums_ref[0:192, :] = total[:, 0:128]
     sums_ref[192:384, 0:64] = total[:, 128:192]
 
     def mid_sum(m, total):
-        return total + dot_t(mx[pl.ds(2 * m, 2)].reshape(192, 128), mc_pad[pl.ds(m, 2)].reshape(128, 128))
-
-    sums_ref[384:576, :] = lax.fori_loop(0, 17, mid_sum, jnp.zeros((192, 128), F32))
+        return total + dot_t(mx[2 * m : 2 * m + 2].reshape(192, 128), mc_pad[m : m + 2].reshape(128, 128))
+
+    total = jnp.zeros((192, 128), F32)
+    for step in range(17):
+        total = mid_sum(step, total)
+    sums_ref[384:576, :] = total
 
     def stem_sum(m, total):
-        return total + dot_t(fx[pl.ds(2 * m, 2)].reshape(192, 256), sc_pad[pl.ds(m, 2)].reshape(64, 256))
-
-    sums_ref[192:384, 64:128] = lax.fori_loop(0, 33, stem_sum, jnp.zeros((192, 64), F32))
+        return total + dot_t(fx[2 * m : 2 * m + 2].reshape(192, 256), sc_pad[m : m + 2].reshape(64, 256))
+
+    total = jnp.zeros((192, 64), F32)
+    for step in range(33):
+        total = stem_sum(step, total)
+    sums_ref[192:384, 64:128] = total
 
     for s in range(SLABS):
         term = sums_ref[s * SHARE : s * SHARE + SHARE, :]
         near = term.astype(BF16).astype(F32)
-        wire_ref[s, COT_ROWS:WIRE_ROWS] = jnp.concatenate([near, term - near], 0).astype(BF16)
+        wire_ref[s, 0:SUM_ROWS] = jnp.concatenate([near, term - near], 0).astype(BF16)
 
 
 def scenario_pass(x, weights, out_weight, cotangent):
@@ -283,10 +294,10 @@
 
 
 def lon_share_kernel(got_ref, out_ref):
-    total = jnp.zeros((2 * SHARE, 128), F32)
+    total = jnp.zeros((SUM_ROWS, 128), F32)
     for k in range(SLABS):
-        total = total + got_ref[k, COT_ROWS:WIRE_ROWS].astype(F32)
-    share = (total[0:SHARE] + total[SHARE : 2 * SHARE]).astype(BF16)
+        total = total + got_ref[k].astype(F32)
+    share = (total[0:SHARE] + total[SHARE:SUM_ROWS]).astype(BF16)
     for k in range(SLABS):
         out_ref[k] = share
 
@@ -335,7 +346,14 @@
 
 def summed_everywhere(got, factor):
     shares = jax.ShapeDtypeStruct((SLABS, SHARE, 128), BF16)
-    share = on_chip(lon_share_kernel, shares, name="lon_share")(got)
+    share = pl.pallas_call(
+        lon_share_kernel,
+        grid=(1,),
+        out_shape=shares,
+        in_specs=[pl.BlockSpec((SLABS, SUM_ROWS, 128), lambda i: (0, 0, 0))],
+        out_specs=pl.BlockSpec((SLABS, SHARE, 128), lambda i: (0, 0, 0)),
+        name="lon_share",
+    )(got)
     share = on_chip(rep_share_kernel, shares, name="rep_share")(exchanged(share, "rep"))
     sums = exchanged(share, "lon").reshape(SLABS * SHARE, 128)
     outs = (
@@ -356,7 +374,7 @@
     prediction, wire = scenario_pass(x, weights, out_weight, cotangent)
     prediction = prediction.reshape(16, 2, 64).transpose(1, 0, 2).reshape(1, 32, 64)
     got = exchanged(wire, "lon")
-    stem_cotangent = got[:, 0:COT_ROWS].reshape(SLABS, C1, 4, 128)
+    stem_cotangent = got[:, SUM_ROWS:].reshape(SLABS, C1, 4, 128)
     factor = 1.0 / (fields.shape[0] * lax.axis_size("rep"))
     return (prediction, stem_cotangent, *summed_everywhere(got, factor))
 

time: 116 us -> 99.7 us (0.86)
  Pallas kernels: 34.1 us -> 17.8 us
    pallas_call x1, Pallas kernels: 28.7 us -> 12.5 us  [scenario_pass(): pl.pallas_call(scenario_kernel, out_shape=out_shape, in_specs=[whole] * 1...]
    pallas_call x3 -> x2, Pallas kernels: 5.43 us -> 3.47 us  [on_chip(): pl.pallas_call(kernel, out_shape=outs, in_specs=[whole] * len(args), out_...]
    pallas_call x0 -> x1, Pallas kernels: none -> 1.77 us  [summed_everywhere(): pl.pallas_call(lon_share_kernel, grid=(1,), out_shape=shares, in_specs=[p...]
  transfers between devices with their start and end apart: 2 -> 2, of which waited for: 2 -> 2; matrix products, arithmetic and copies ran while one was open for 5% -> 6% of each run, Pallas kernels for 0% -> 0%
where the time goes in v2:
time: 99.7 us; the launch traced here: 99.2 us
  blocking collectives  39 us (39%)
  waiting for transfers between devices  21.5 us (22%)
  Pallas kernels  17.8 us (18%)
  starting transfers between devices  12.8 us (13%)
  local copies, waits for them, and re-layouts  4.93 us (5%)
  other arithmetic  2.16 us (2%)
  between operations  1.06 us (1%)
    all_to_all x2, blocking collectives, exchanged(): return lax.all_to_all(value, axis, split_axis=0, concat_axis=0, tiled=True)  39 us
    all_to_all x2, waiting for transfers between devices, exchanged(): return lax.all_to_all(value, axis, split_axis=0, concat_axis=0, tiled=True)  21.5 us
    all_to_all x2, starting transfers between devices, exchanged(): return lax.all_to_all(value, axis, split_axis=0, concat_axis=0, tiled=True)  12.8 us
    pallas_call x1, Pallas kernels, scenario_pass(): pl.pallas_call(scenario_kernel, out_shape=out_shape, in_specs=[whole] * 1...  12.5 us
    pallas_call x2, Pallas kernels, on_chip(): pl.pallas_call(kernel, out_shape=outs, in_specs=[whole] * len(args), out_...  3.47 us
  transfers between devices with their start and end apart: 2, of which 2 were waited for; matrix products, arithmetic and copies ran while one was open for 6% of the time, Pallas kernels for 0%

profile of v2, /device:TPU:1, one launch (start us, length us, event | category | flops | bytes accessed | tf_op | source)
XLA Modules:
  0.0 99.2 jit_solution(17114911485656704969)
XLA Ops:
  0.6 0.0 copy-start.5
  0.6 0.0 copy-start.6
  0.7 0.0 copy-start.4
  0.7 0.0 copy-start.2
  0.7 7.1 %all-to-all-start = ((bf16[16,192,256]{2,1,0:T(8,128)(2,1)}), bf16[16,192,256]{2,1,0:T(8,128)(2,1)S(1)}, u32[]{:S(2)}, u32[]{:S(2)}) async-start(bf16[16,192,256]{2,1,0:T(8,128)(2,1)} %bitcast.81), calls=%async_computation | async-start | bytes 3145728 | tf_op jit(solution)/shard_map/all_to_all | solution.py:293
  8.0 0.0 copy-done.5
  8.1 0.1 reshape.74.pc_ref
  8.1 0.0 copy-done.6
  8.1 0.1 copy.53.ow_ref
  8.2 0.0 copy-done.4
  8.2 0.2 copy.42
  8.4 0.1 reshape.64
  8.6 0.1 copy.47
  8.7 0.2 copy.49
  8.9 0.1 pad_bitcast_fusion.3
  9.0 0.2 pad_maximum_fusion.2
  9.3 0.0 copy-start.3
  9.3 0.2 reshape.71.w3b_ref
  9.5 0.1 pad_bitcast_fusion.1
  9.6 0.1 pad_maximum_fusion
  9.7 0.2 copy.48
  9.9 0.2 reshape.69.w3_ref
  10.2 0.1 pad_maximum_fusion.3
  10.3 0.2 copy.56
  10.5 0.2 reshape.80.w2_ref
  10.7 0.1 pad_maximum_fusion.1
  10.8 0.2 copy.43
  11.0 0.4 reshape.65.w1_ref
  11.4 0.1 fusion.18.w2b_ref
  11.5 0.2 select_convert_fusion.4.rows_ref
  11.7 0.2 select_convert_fusion.3.regroup_ref
  11.9 0.8 select_convert_fusion.2.inter_ref
  12.6 0.3 select_convert_fusion.1.staps_ref
  12.9 0.1 select_convert_fusion.ftaps_ref
  13.0 16.5 %all-to-all-done.x_ref = bf16[16,192,256]{2,1,0:T(8,128)(2,1)S(1)} async-done(((bf16[16,192,256]{2,1,0:T(8,128)(2,1)}), bf16[16,192,256]{2,1,0:T(8,128)(2,1)S(1)}, u32[]{:S(2)}, u32[]{:S(2)}) %all-to-all-start) | async-done | bytes 1572896 | tf_op jit(solution)/shard_map/all_to_all | solution.py:293
  29.5 12.5 %scenario.1 = (f32[16,128]{1,0:T(8,128)S(1)}, bf16[16,208,128]{2,1,0:T(8,128)(2,1)S(1)}) custom-call(bf16[16,192,256]{2,1,0:T(8,128)(2,1)S(1)} %all-to-all-done.x_ref, bf16[128,960]{1,0:T(8,128)(2,1)S(1)} %reshape.65.w1_ref, bf16[128,480]{1,0:T(8,128)(2,1)S(1)} %reshape.80.w2_ref, bf16[128,768]{1,0:T(8,128)(2,1)S(1)} %reshape.69.w3_ref, ...), custom_call_target="tpu_custom_call" | custom-call | flops 4000000000 | bytes 4194304 | tf_op jit(solution)/shard_map/scenario/pallas_call | solution.py:280
  42.1 18.0 %all_to_all.20.got_ref = bf16[16,208,128]{2,1,0:T(8,128)(2,1)} all-to-all(bf16[16,208,128]{2,1,0:T(8,128)(2,1)S(1)} %get-tuple-element.13), channel_id=1, replica_groups=mesh['lon'=16,'rep'=16] {'lon'}, dimensions={0} | all-to-all | bytes 1703936 | tf_op jit(solution)/shard_map/all_to_all | solution.py:293
  60.1 1.8 %lon_share.1 = bf16[16,40,128]{2,1,0:T(8,128)(2,1)} custom-call(bf16[16,208,128]{2,1,0:T(8,128)(2,1)} %all_to_all.20.got_ref), custom_call_target="tpu_custom_call" | custom-call | tf_op jit(solution)/shard_map/lon_share/pallas_call | solution.py:349
  61.9 20.9 %all_to_all.21.got_ref = bf16[16,40,128]{2,1,0:T(8,128)(2,1)} all-to-all(bf16[16,40,128]{2,1,0:T(8,128)(2,1)} %lon_share.1), channel_id=1, replica_groups=mesh['lon'=16,'rep'=16] {'rep'}, dimensions={0} | all-to-all | bytes 327680 | tf_op jit(solution)/shard_map/all_to_all | solution.py:293
  82.8 1.6 %rep_share.1 = bf16[16,40,128]{2,1,0:T(8,128)(2,1)} custom-call(bf16[16,40,128]{2,1,0:T(8,128)(2,1)} %all_to_all.21.got_ref), custom_call_target="tpu_custom_call" | custom-call | tf_op jit(solution)/shard_map/rep_share/pallas_call | solution.py:337
  84.4 5.8 %all-to-all-start.3 = ((bf16[16,40,128]{2,1,0:T(8,128)(2,1)}), bf16[16,40,128]{2,1,0:T(8,128)(2,1)S(1)}, u32[]{:S(2)}, u32[]{:S(2)}) async-start(bf16[16,40,128]{2,1,0:T(8,128)(2,1)} %rep_share.1), calls=%async_computation.3 | async-start | bytes 327680 | tf_op jit(solution)/shard_map/all_to_all | solution.py:293
  90.2 0.1 reshape.75
  90.3 0.6 copy.54
  90.9 0.0 copy-done
  90.9 0.8 slice.40
  91.7 5.0 %all-to-all-done.3 = bf16[16,40,128]{2,1,0:T(8,128)(2,1)S(1)} async-done(((bf16[16,40,128]{2,1,0:T(8,128)(2,1)}), bf16[16,40,128]{2,1,0:T(8,128)(2,1)S(1)}, u32[]{:S(2)}, u32[]{:S(2)}) %all-to-all-start.3) | async-done | bytes 163872 | tf_op jit(solution)/shard_map/all_to_all | solution.py:293
  96.7 0.7 copy-done.1
  97.4 1.9 %unpack.1 = (f32[24,4,4,32]{3,2,1,0:T(4,128)}, f32[3,3,32,64]{3,2,1,0:T(8,128)}, f32[3,3,64,64]{3,2,1,0:T(8,128)}, f32[1,64]{1,0:T(1,128)}) custom-call(bf16[640,128]{1,0:T(8,128)(2,1)} %bitcast.82), custom_call_target="tpu_custom_call" | custom-call | tf_op jit(solution)/shard_map/unpack/pallas_call | solution.py:337
  (36 shorter events, 0.3 us)
Async XLA Ops:
  0.6 7.4 %copy-start.5 = (f32[1,32,64]{2,1,0:T(8,128)S(1)}, f32[1,32,64]{2,1,0:T(8,128)}, u32[]{:S(2)}) copy-start(f32[1,32,64]{2,1,0:T(8,128)} %param.11) | copy-start | bytes 24580
  0.6 7.5 %copy-start.6 = (f32[64]{0:T(128)S(1)}, f32[64]{0:T(128)}, u32[]{:S(2)}) copy-start(f32[64]{0:T(128)} %param.10) | copy-start | bytes 772
  0.7 7.6 %copy-start.4 = (bf16[32,24,4,4]{0,3,2,1:T(4,128)(2,1)S(1)}, bf16[32,24,4,4]{0,3,2,1:T(4,128)(2,1)}, u32[]{:S(2)}) copy-start(bf16[32,24,4,4]{0,3,2,1:T(4,128)(2,1)} %param.7) | copy-start | bytes 73732
  0.7 7.9 %copy-start.2 = (bf16[64,64,3,3]{1,0,3,2:T(8,128)(2,1)S(1)}, bf16[64,64,3,3]{1,0,3,2:T(8,128)(2,1)}, u32[]{:S(2)}) copy-start(bf16[64,64,3,3]{1,0,3,2:T(8,128)(2,1)} %param.9) | copy-start | bytes 221188
  0.7 28.9 %all-to-all-start = ((bf16[16,192,256]{2,1,0:T(8,128)(2,1)}), bf16[16,192,256]{2,1,0:T(8,128)(2,1)S(1)}, u32[]{:S(2)}, u32[]{:S(2)}) async-start(bf16[16,192,256]{2,1,0:T(8,128)(2,1)} %bitcast.81), calls=%async_computation | async-start | bytes 3145728 | tf_op jit(solution)/shard_map/all_to_all | solution.py:293
  9.3 0.9 copy-start.3
  60.1 30.8 %copy-start = (bf16[16,208,128]{2,1,0:T(8,128)(2,1)S(1)}, bf16[16,208,128]{2,1,0:T(8,128)(2,1)}, u32[]{:S(2)}) copy-start(bf16[16,208,128]{2,1,0:T(8,128)(2,1)} %all_to_all.20.got_ref) | copy-start | bytes 2555908
  84.4 12.3 %all-to-all-start.3 = ((bf16[16,40,128]{2,1,0:T(8,128)(2,1)}), bf16[16,40,128]{2,1,0:T(8,128)(2,1)S(1)}, u32[]{:S(2)}, u32[]{:S(2)}) async-start(bf16[16,40,128]{2,1,0:T(8,128)(2,1)} %rep_share.1), calls=%async_computation.3 | async-start | bytes 327680 | tf_op jit(solution)/shard_map/all_to_all | solution.py:293
  96.7 0.7 copy-start.1

commit v3 on v2

--- a/solution.py
+++ b/solution.py
@@ -11,9 +11,9 @@
 SLABS, CIN, SLAB_LON, LAT = 16, 24, 8, 256
 C1, C2 = 32, 64
 COT_ROWS, SHARE = 128, 40
-SUM_ROWS = 2 * SHARE
-WIRE_ROWS = SUM_ROWS + COT_ROWS
-STEM_GROUP, MID_GROUP, HEAD_GROUP = 4, 2, 2
+WIRE_ROWS = SHARE + COT_ROWS
+STEM_GROUP, STEM_BATCH, MID_GROUP, HEAD_GROUP = 4, 4, 2, 2
+SLAB_BATCH, BACK_BATCH = 2, 8
 
 
 def one_hot(shape, test):
@@ -36,8 +36,7 @@
         (256, 256),
         lambda r, c: (r % 128 // 64 == c // 128) & (c % 128 == 2 * (r % 64) + r // 128),
     )
-    slab_rows = one_hot((128, 128), lambda r, c: (r % 4 == c // C1) & (r // 4 == c % C1))
-    return regroup, field_taps, stem_taps, interleave, slab_rows
+    return regroup, field_taps, stem_taps, interleave
 
 
 def toeplitz(rows, group, step):
@@ -100,7 +99,7 @@
 
 
 def scenario_kernel(
-    x_ref, w1_ref, w2_ref, w3_ref, w3b_ref, w2b_ref, regroup_ref, ftaps_ref, staps_ref, inter_ref, rows_ref,
+    x_ref, w1_ref, w2_ref, w3_ref, w3b_ref, w2b_ref, regroup_ref, ftaps_ref, staps_ref, inter_ref,
     ow_ref, pc_ref,
     pred_ref, wire_ref,
     sums_ref, fx, stem_pre, mx, mid_pre, hx, hc_wide, hc_pad, mc_pair, mc_pad, sc_pad,
@@ -114,17 +113,20 @@
     def later(block):
         return jnp.where(last, 0.0, pltpu.roll(block, 127, 1))
 
-    def load_slab(s):
-        for half in (0, 1):
-            part = dot(regroup_ref[...], x_ref[s + 8 * half]).astype(BF16)
-            taps = dot(part, ftaps_ref[...])
+    def load_slabs(at):
+        places = [(s, half) for s in range(at, at + SLAB_BATCH) for half in (0, 1)]
+        parts = [dot(regroup_ref[...], x_ref[s + 8 * half]).astype(BF16) for s, half in places]
+        all_taps = dot(jnp.concatenate(parts, 0), ftaps_ref[...])
+        for k, (s, half) in enumerate(places):
+            taps = all_taps[192 * k : 192 * k + 192]
             wide = jnp.concatenate(
                 [taps[:, 128 * b : 128 * b + 128].reshape(SLAB_LON, CIN, 128) for b in range(4)], 1
             )
-            fx[1 + s * SLAB_LON : 1 + s * SLAB_LON + SLAB_LON, :, half * 128 : half * 128 + 128] = wide.astype(BF16)
-
-    for step in range(8):
-        load_slab(step)
+            rows = slice(1 + s * SLAB_LON, 1 + s * SLAB_LON + SLAB_LON)
+            fx[rows, :, half * 128 : half * 128 + 128] = wide.astype(BF16)
+
+    for at in range(0, 8, SLAB_BATCH):
+        load_slabs(at)
     fx[0, :, 0:128] = fx[64, :, 128:256]
     fx[0, :, 128:256] = fx[64, :, 0:128]
     fx[65, :, 0:128] = fx[1, :, 128:256]
@@ -135,13 +137,16 @@
         window = fx[pl.ds(2 * n * g, 2 * n + 2)].reshape((2 * n + 2) * 96, 256)
         pre = dot(w1_ref[...], window)
         stem_pre[n * g : n * g + n] = pre.reshape(n, C1, 256)
-        act = (pre * sigmoid(pre)).astype(BF16)
-        taps = dot(act, staps_ref[...])
+        return (pre * sigmoid(pre)).astype(BF16)
+
+    def stem_taps(acts, at):
+        n = STEM_GROUP * len(acts)
+        taps = dot(jnp.concatenate(acts, 0), staps_ref[...])
         wide = jnp.concatenate([taps[:, 128 * b : 128 * b + 128].reshape(n, C1, 128) for b in range(3)], 1)
-        mx[1 + n * g : 1 + n * g + n] = wide.astype(BF16)
-
-    for step in range(32 // STEM_GROUP):
-        stem(step)
+        mx[1 + at : 1 + at + n] = wide.astype(BF16)
+
+    for at in range(0, 32 // STEM_GROUP, STEM_BATCH):
+        stem_taps([stem(at + k) for k in range(STEM_BATCH)], at * STEM_GROUP)
     mx[0] = swapped(mx[32])
     mx[33] = jnp.zeros((96, 128), BF16)
 
@@ -209,21 +214,22 @@
     for edge in (0, 33):
         sc_pad[edge] = jnp.zeros((C1, 256), BF16)
 
-    def mid_back(m):
+    def mid_back(at):
         parts = []
-        for k in range(2):
-            window = mc_pair[2 * m + k : 2 * m + k + 2].reshape(256, 128)
+        for r in range(at, at + BACK_BATCH):
+            window = mc_pair[r : r + 2].reshape(256, 128)
             grad = dot(w2b_ref[...], window).astype(BF16)
             parts.append(jnp.concatenate([grad[0:64], grad[64:128]], 1))
-        grad = dot(jnp.concatenate(parts, 0), inter_ref[...])
-        cot = (grad * slope_of(stem_pre[4 * m : 4 * m + 4].reshape(128, 256))).astype(BF16)
-        sc_pad[4 * m + 1 : 4 * m + 1 + 4] = cot.reshape(4, C1, 256)
-        out = dot(rows_ref[...], cot).astype(BF16)
-        wire_ref[m, SUM_ROWS:WIRE_ROWS] = out[:, 0:128]
-        wire_ref[m + 8, SUM_ROWS:WIRE_ROWS] = out[:, 128:256]
-
-    for step in range(8):
-        mid_back(step)
+        grads = dot(jnp.concatenate(parts, 0), inter_ref[...])
+        for m in range(at // 2, (at + BACK_BATCH) // 2):
+            grad = grads[128 * m - 64 * at : 128 * m - 64 * at + 128]
+            cot = (grad * slope_of(stem_pre[4 * m : 4 * m + 4].reshape(128, 256))).astype(BF16)
+            sc_pad[4 * m + 1 : 4 * m + 5] = cot.reshape(4, C1, 256)
+            wire_ref[m, SHARE:WIRE_ROWS] = cot[:, 0:128]
+            wire_ref[m + 8, SHARE:WIRE_ROWS] = cot[:, 128:256]
+
+    for at in range(0, 16, BACK_BATCH):
+        mid_back(at)
 
     def head_sum(p, total):
         left = jnp.concatenate([hc_pad[2 * p + k : 2 * p + k + 3].reshape(192, 128) for k in range(2)], 1)
@@ -253,9 +259,7 @@
     sums_ref[192:384, 64:128] = total
 
     for s in range(SLABS):
-        term = sums_ref[s * SHARE : s * SHARE + SHARE, :]
-        near = term.astype(BF16).astype(F32)
-        wire_ref[s, 0:SUM_ROWS] = jnp.concatenate([near, term - near], 0).astype(BF16)
+        wire_ref[s, 0:SHARE] = sums_ref[s * SHARE : s * SHARE + SHARE, :].astype(BF16)
 
 
 def scenario_pass(x, weights, out_weight, cotangent):
@@ -280,10 +284,10 @@
     return pl.pallas_call(
         scenario_kernel,
         out_shape=out_shape,
-        in_specs=[whole] * 13,
+        in_specs=[whole] * 12,
         out_specs=(whole,) * 2,
         scratch_shapes=scratch,
-        compiler_params=pltpu.CompilerParams(vmem_limit_bytes=48 << 20),
+        compiler_params=pltpu.CompilerParams(vmem_limit_bytes=32 << 20),
         cost_estimate=pl.CostEstimate(flops=4 * 10**9, bytes_accessed=4 << 20, transcendentals=10**6),
         name="scenario",
     )(x, *weights, *selections(), out_weight.reshape(C2, 1), cotangent)
@@ -293,19 +297,10 @@
     return lax.all_to_all(value, axis, split_axis=0, concat_axis=0, tiled=True)
 
 
-def lon_share_kernel(got_ref, out_ref):
-    total = jnp.zeros((SUM_ROWS, 128), F32)
-    for k in range(SLABS):
-        total = total + got_ref[k].astype(F32)
-    share = (total[0:SHARE] + total[SHARE:SUM_ROWS]).astype(BF16)
-    for k in range(SLABS):
-        out_ref[k] = share
-
-
-def rep_share_kernel(got_ref, out_ref):
+def share_kernel(got_ref, out_ref):
     total = jnp.zeros((SHARE, 128), F32)
     for k in range(SLABS):
-        total = total + got_ref[k].astype(F32)
+        total = total + got_ref[k, 0:SHARE].astype(F32)
     share = total.astype(BF16)
     for k in range(SLABS):
         out_ref[k] = share
@@ -340,21 +335,15 @@
         in_specs=[whole] * len(args),
         out_specs=whole if single else (whole,) * len(outs),
         scratch_shapes=scratch,
+        compiler_params=pltpu.CompilerParams(vmem_limit_bytes=8 << 20),
         name=name,
     )(*args)
 
 
 def summed_everywhere(got, factor):
     shares = jax.ShapeDtypeStruct((SLABS, SHARE, 128), BF16)
-    share = pl.pallas_call(
-        lon_share_kernel,
-        grid=(1,),
-        out_shape=shares,
-        in_specs=[pl.BlockSpec((SLABS, SUM_ROWS, 128), lambda i: (0, 0, 0))],
-        out_specs=pl.BlockSpec((SLABS, SHARE, 128), lambda i: (0, 0, 0)),
-        name="lon_share",
-    )(got)
-    share = on_chip(rep_share_kernel, shares, name="rep_share")(exchanged(share, "rep"))
+    share = on_chip(share_kernel, shares, name="lon_share")(got)
+    share = on_chip(share_kernel, shares, name="rep_share")(exchanged(share, "rep"))
     sums = exchanged(share, "lon").reshape(SLABS * SHARE, 128)
     outs = (
         jax.ShapeDtypeStruct((CIN, 4, 4, C1), F32),
@@ -374,7 +363,7 @@
     prediction, wire = scenario_pass(x, weights, out_weight, cotangent)
     prediction = prediction.reshape(16, 2, 64).transpose(1, 0, 2).reshape(1, 32, 64)
     got = exchanged(wire, "lon")
-    stem_cotangent = got[:, SUM_ROWS:].reshape(SLABS, C1, 4, 128)
+    stem_cotangent = got[:, SHARE:].reshape(SLABS, 4, C1, 128).transpose(0, 2, 1, 3)
     factor = 1.0 / (fields.shape[0] * lax.axis_size("rep"))
     return (prediction, stem_cotangent, *summed_everywhere(got, factor))
 

time: 99.7 us -> 88.9 us (0.89)
  Pallas kernels: 17.8 us -> 9.58 us
  blocking collectives: 39 us -> 37.2 us
    pallas_call x1, Pallas kernels: 12.5 us -> 7.91 us  [scenario_pass(): pl.pallas_call(scenario_kernel, out_shape=out_shape, in_specs=[whole] * 1...]
    pallas_call x2 -> x3, Pallas kernels: 3.47 us -> 1.68 us  [on_chip(): pl.pallas_call(kernel, out_shape=outs, in_specs=[whole] * len(args), out_...]
    pallas_call x1 -> x0, Pallas kernels: 1.77 us -> none  [summed_everywhere(): pl.pallas_call(lon_share_kernel, grid=(1,), out_shape=shares, in_specs=[p...]
    all_to_all x2, blocking collectives: 39 us -> 37.2 us  [exchanged(): return lax.all_to_all(value, axis, split_axis=0, concat_axis=0, tiled=True)]
    reshape x0 -> x1, local copies, waits for them, and re-layouts: none -> 1.07 us  [local(): got[:, SHARE:].reshape(SLABS, 4, C1, 128).transpose(0, 2, 1, 3)]
  transfers between devices with their start and end apart: 2 -> 2, of which waited for: 2 -> 2; matrix products, arithmetic and copies ran while one was open for 6% -> 7% of each run, Pallas kernels for 0% -> 0%
where the time goes in v3:
time: 88.9 us; the launch traced here: 88.6 us
  blocking collectives  37.2 us (42%)
  waiting for transfers between devices  21.6 us (24%)
  starting transfers between devices  12.8 us (14%)
  Pallas kernels  9.58 us (11%)
  local copies, waits for them, and re-layouts  4.53 us (5%)
  other arithmetic  1.78 us (2%)
  between operations  1.02 us (1%)
    all_to_all x2, blocking collectives, exchanged(): return lax.all_to_all(value, axis, split_axis=0, concat_axis=0, tiled=True)  37.2 us
    all_to_all x2, waiting for transfers between devices, exchanged(): return lax.all_to_all(value, axis, split_axis=0, concat_axis=0, tiled=True)  21.6 us
    all_to_all x2, starting transfers between devices, exchanged(): return lax.all_to_all(value, axis, split_axis=0, concat_axis=0, tiled=True)  12.8 us
    pallas_call x1, Pallas kernels, scenario_pass(): pl.pallas_call(scenario_kernel, out_shape=out_shape, in_specs=[whole] * 1...  7.91 us
  transfers between devices with their start and end apart: 2, of which 2 were waited for; matrix products, arithmetic and copies ran while one was open for 7% of the time, Pallas kernels for 0%

profile of v3, /device:TPU:1, one launch (start us, length us, event | category | flops | bytes accessed | tf_op | source)
XLA Modules:
  0.0 88.6 jit_solution(8659139775806114869)
XLA Ops:
  0.6 0.0 copy-start.3
  0.6 0.0 copy-start.4
  0.7 0.0 copy-start.2
  0.7 0.0 copy-start
  0.7 7.1 %all-to-all-start = ((bf16[16,192,256]{2,1,0:T(8,128)(2,1)}), bf16[16,192,256]{2,1,0:T(8,128)(2,1)S(1)}, u32[]{:S(2)}, u32[]{:S(2)}) async-start(bf16[16,192,256]{2,1,0:T(8,128)(2,1)} %bitcast.86), calls=%async_computation | async-start | bytes 3145728 | tf_op jit(solution)/shard_map/all_to_all | solution.py:297
  7.9 0.0 copy-done.3
  8.0 0.1 reshape.74.pc_ref
  8.0 0.0 copy-done.4
  8.0 0.1 copy.56.ow_ref
  8.1 0.0 copy-done.2
  8.1 0.2 copy.45
  8.3 0.1 reshape.64
  8.5 0.0 copy-done
  8.5 0.1 copy.50
  8.6 0.2 copy.52
  8.8 0.1 pad_bitcast_fusion.3
  9.0 0.2 pad_maximum_fusion.2
  9.2 0.0 copy-start.1
  9.2 0.2 reshape.71.w3b_ref
  9.4 0.1 pad_bitcast_fusion.1
  9.5 0.1 pad_maximum_fusion
  9.6 0.2 copy.51
  9.8 0.2 reshape.69.w3_ref
  10.1 0.0 copy-done.1
  10.1 0.1 pad_maximum_fusion.3
  10.2 0.2 copy.60
  10.4 0.2 reshape.80.w2_ref
  10.6 0.1 pad_maximum_fusion.1
  10.7 0.2 copy.46
  10.9 0.4 reshape.65.w1_ref
  11.3 0.1 fusion.18.w2b_ref
  11.4 0.2 select_convert_fusion.3.regroup_ref
  11.6 0.6 select_convert_fusion.2.inter_ref
  12.2 0.3 select_convert_fusion.1.staps_ref
  12.5 0.1 select_convert_fusion.ftaps_ref
  12.6 17.0 %all-to-all-done.x_ref = bf16[16,192,256]{2,1,0:T(8,128)(2,1)S(1)} async-done(((bf16[16,192,256]{2,1,0:T(8,128)(2,1)}), bf16[16,192,256]{2,1,0:T(8,128)(2,1)S(1)}, u32[]{:S(2)}, u32[]{:S(2)}) %all-to-all-start) | async-done | bytes 1572896 | tf_op jit(solution)/shard_map/all_to_all | solution.py:297
  29.5 7.9 %scenario.1 = (f32[16,128]{1,0:T(8,128)S(1)}, bf16[16,168,128]{2,1,0:T(8,128)(2,1)S(1)}) custom-call(bf16[16,192,256]{2,1,0:T(8,128)(2,1)S(1)} %all-to-all-done.x_ref, bf16[128,960]{1,0:T(8,128)(2,1)S(1)} %reshape.65.w1_ref, bf16[128,480]{1,0:T(8,128)(2,1)S(1)} %reshape.80.w2_ref, bf16[128,768]{1,0:T(8,128)(2,1)S(1)} %reshape.69.w3_ref, ...), custom_call_target="tpu_custom_call" | custom-call | flops 4000000000 | bytes 4194304 | tf_op jit(solution)/shard_map/scenario/pallas_call | solution.py:284
  37.4 16.7 %all_to_all.20.got_ref = bf16[16,168,128]{2,1,0:T(8,128)(2,1)S(1)} all-to-all(bf16[16,168,128]{2,1,0:T(8,128)(2,1)S(1)} %get-tuple-element.13), channel_id=1, replica_groups=mesh['lon'=16,'rep'=16] {'lon'}, dimensions={0} | all-to-all | bytes 1376256 | tf_op jit(solution)/shard_map/all_to_all | solution.py:297
  54.1 20.5 %all_to_all.21.got_ref = bf16[16,40,128]{2,1,0:T(8,128)(2,1)S(1)} all-to-all(bf16[16,40,128]{2,1,0:T(8,128)(2,1)S(1)} %lon_share.1), channel_id=1, replica_groups=mesh['lon'=16,'rep'=16] {'rep'}, dimensions={0} | all-to-all | bytes 327680 | tf_op jit(solution)/shard_map/all_to_all | solution.py:297
  74.7 0.7 rep_share.1
  75.4 5.8 %all-to-all-start.3 = ((bf16[16,40,128]{2,1,0:T(8,128)(2,1)}), bf16[16,40,128]{2,1,0:T(8,128)(2,1)S(1)}, u32[]{:S(2)}, u32[]{:S(2)}) async-start(bf16[16,40,128]{2,1,0:T(8,128)(2,1)} %rep_share.1), calls=%async_computation.3 | async-start | bytes 327680 | tf_op jit(solution)/shard_map/all_to_all | solution.py:297
  81.1 0.1 reshape.75
  81.2 0.6 copy.57
  81.8 1.1 %copy.64 = bf16[16,4,32,128]{3,1,2,0:T(4,128)(2,1)} copy(bf16[16,4,32,128]{3,2,1,0:T(8,128)(2,1)S(1)} %bitcast.85) | data formatting | bytes 1048576 | tf_op jit(solution)/shard_map/reshape | solution.py:366
  82.9 4.7 %all-to-all-done.3 = bf16[16,40,128]{2,1,0:T(8,128)(2,1)S(1)} async-done(((bf16[16,40,128]{2,1,0:T(8,128)(2,1)}), bf16[16,40,128]{2,1,0:T(8,128)(2,1)S(1)}, u32[]{:S(2)}, u32[]{:S(2)}) %all-to-all-start.3) | async-done | bytes 163872 | tf_op jit(solution)/shard_map/all_to_all | solution.py:297
  87.6 0.9 %unpack.1 = (f32[24,4,4,32]{3,2,1,0:T(4,128)}, f32[3,3,32,64]{3,2,1,0:T(8,128)}, f32[3,3,64,64]{3,2,1,0:T(8,128)}, f32[1,64]{1,0:T(1,128)}) custom-call(bf16[640,128]{1,0:T(8,128)(2,1)S(1)} %bitcast.84), custom_call_target="tpu_custom_call" | custom-call | tf_op jit(solution)/shard_map/unpack/pallas_call | solution.py:332
  (28 shorter events, 0.3 us)
Async XLA Ops:
  0.6 7.3 %copy-start.3 = (f32[1,32,64]{2,1,0:T(8,128)S(1)}, f32[1,32,64]{2,1,0:T(8,128)}, u32[]{:S(2)}) copy-start(f32[1,32,64]{2,1,0:T(8,128)} %param.11) | copy-start | bytes 24580
  0.6 7.4 %copy-start.4 = (f32[64]{0:T(128)S(1)}, f32[64]{0:T(128)}, u32[]{:S(2)}) copy-start(f32[64]{0:T(128)} %param.10) | copy-start | bytes 772
  0.7 7.5 %copy-start.2 = (bf16[32,24,4,4]{0,3,2,1:T(4,128)(2,1)S(1)}, bf16[32,24,4,4]{0,3,2,1:T(4,128)(2,1)}, u32[]{:S(2)}) copy-start(bf16[32,24,4,4]{0,3,2,1:T(4,128)(2,1)} %param.7) | copy-start | bytes 73732
  0.7 7.8 %copy-start = (bf16[64,64,3,3]{1,0,3,2:T(8,128)(2,1)S(1)}, bf16[64,64,3,3]{1,0,3,2:T(8,128)(2,1)}, u32[]{:S(2)}) copy-start(bf16[64,64,3,3]{1,0,3,2:T(8,128)(2,1)} %param.9) | copy-start | bytes 221188
  0.7 28.9 %all-to-all-start = ((bf16[16,192,256]{2,1,0:T(8,128)(2,1)}), bf16[16,192,256]{2,1,0:T(8,128)(2,1)S(1)}, u32[]{:S(2)}, u32[]{:S(2)}) async-start(bf16[16,192,256]{2,1,0:T(8,128)(2,1)} %bitcast.86), calls=%async_computation | async-start | bytes 3145728 | tf_op jit(solution)/shard_map/all_to_all | solution.py:297
  9.2 0.9 %copy-start.1 = (bf16[64,32,3,3]{0,1,3,2:T(8,128)(2,1)S(1)}, bf16[64,32,3,3]{0,1,3,2:T(8,128)(2,1)}, u32[]{:S(2)}) copy-start(bf16[64,32,3,3]{0,1,3,2:T(8,128)(2,1)} %param.8) | copy-start | bytes 110596
  75.4 12.3 %all-to-all-start.3 = ((bf16[16,40,128]{2,1,0:T(8,128)(2,1)}), bf16[16,40,128]{2,1,0:T(8,128)(2,1)S(1)}, u32[]{:S(2)}, u32[]{:S(2)}) async-start(bf16[16,40,128]{2,1,0:T(8,128)(2,1)} %rep_share.1), calls=%async_computation.3 | async-start | bytes 327680 | tf_op jit(solution)/shard_map/all_to_all | solution.py:297

commit v4 on v3

--- a/solution.py
+++ b/solution.py
@@ -27,10 +27,10 @@
         (CIN * SLAB_LON, CIN * SLAB_LON),
         lambda r, c: (r % CIN == c // SLAB_LON) & (r // CIN == c % SLAB_LON),
     )
-    field_taps = one_hot((LAT, 512), lambda r, c: r == 2 * (c % 128) + c // 128 - 1)
+    field_taps = one_hot((LAT, 256), lambda r, c: r == 2 * (c % 128) + c // 128)
     stem_taps = one_hot(
-        (256, 384),
-        lambda r, c: (r // 128 == c % 128 // 64) & (r % 128 == 2 * (c % 64) + c // 128 - 1),
+        (256, 256),
+        lambda r, c: (r // 128 == c % 128 // 64) & (r % 128 == 2 * (c % 64) + c // 128),
     )
     interleave = one_hot(
         (256, 256),
@@ -85,6 +85,10 @@
     return lax.dot_general(left, right, (((1,), (1,)), ((), ())), preferred_element_type=F32)
 
 
+def turned(block):
+    return block.astype(F32).T.astype(BF16)
+
+
 def swapped(block):
     return pltpu.roll(block.astype(F32), 64, 1).astype(BF16)
 
@@ -113,15 +117,18 @@
     def later(block):
         return jnp.where(last, 0.0, pltpu.roll(block, 127, 1))
 
+    lat = lax.broadcasted_iota(jnp.int32, (192, 128), 1)
+
     def load_slabs(at):
         places = [(s, half) for s in range(at, at + SLAB_BATCH) for half in (0, 1)]
         parts = [dot(regroup_ref[...], x_ref[s + 8 * half]).astype(BF16) for s, half in places]
         all_taps = dot(jnp.concatenate(parts, 0), ftaps_ref[...])
         for k, (s, half) in enumerate(places):
             taps = all_taps[192 * k : 192 * k + 192]
-            wide = jnp.concatenate(
-                [taps[:, 128 * b : 128 * b + 128].reshape(SLAB_LON, CIN, 128) for b in range(4)], 1
-            )
+            even, odd = taps[:, 0:128], taps[:, 128:256]
+            before = jnp.where(lat == 0, 0.0, pltpu.roll(odd, 1, 1))
+            after = jnp.where(lat == 127, 0.0, pltpu.roll(even, 127, 1))
+            wide = jnp.concatenate([t.reshape(SLAB_LON, CIN, 128) for t in (before, even, odd, after)], 1)
             rows = slice(1 + s * SLAB_LON, 1 + s * SLAB_LON + SLAB_LON)
             fx[rows, :, half * 128 : half * 128 + 128] = wide.astype(BF16)
 
@@ -142,7 +149,10 @@
     def stem_taps(acts, at):
         n = STEM_GROUP * len(acts)
         taps = dot(jnp.concatenate(acts, 0), staps_ref[...])
-        wide = jnp.concatenate([taps[:, 128 * b : 128 * b + 128].reshape(n, C1, 128) for b in range(3)], 1)
+        even, odd = taps[:, 0:128], taps[:, 128:256]
+        lat = lax.broadcasted_iota(jnp.int32, odd.shape, 1) % 64
+        before = jnp.where(lat == 0, 0.0, pltpu.roll(odd, 1, 1))
+        wide = jnp.concatenate([t.reshape(n, C1, 128) for t in (before, even, odd)], 1)
         mx[1 + at : 1 + at + n] = wide.astype(BF16)
 
     for at in range(0, 32 // STEM_GROUP, STEM_BATCH):
@@ -231,33 +241,24 @@
     for at in range(0, 16, BACK_BATCH):
         mid_back(at)
 
-    def head_sum(p, total):
-        left = jnp.concatenate([hc_pad[2 * p + k : 2 * p + k + 3].reshape(192, 128) for k in range(2)], 1)
-        right = jnp.concatenate([hx[2 * p], hx[2 * p + 1]], 1)
-        return total + dot_t(left, right)
-
-    total = jnp.zeros((192, 192), F32)
-    for step in range(9):
-        total = head_sum(step, total)
+    total = None
+    for k in range(0, 18, 2):
+        left = jnp.concatenate([hc_pad[j : j + 3].reshape(192, 128) for j in (k, k + 1)], 1)
+        right = jnp.concatenate([turned(hx[j]) for j in (k, k + 1)], 0)
+        term = dot(left, right)
+        total = term if total is None else total + term
     sums_ref[0:192, :] = total[:, 0:128]
     sums_ref[192:384, 0:64] = total[:, 128:192]
-
-    def mid_sum(m, total):
-        return total + dot_t(mx[2 * m : 2 * m + 2].reshape(192, 128), mc_pad[m : m + 2].reshape(128, 128))
-
-    total = jnp.zeros((192, 128), F32)
-    for step in range(17):
-        total = mid_sum(step, total)
+    total = None
+    for k in range(17):
+        term = dot_t(mx[2 * k : 2 * k + 2].reshape(192, 128), mc_pad[k : k + 2].reshape(128, 128))
+        total = term if total is None else total + term
     sums_ref[384:576, :] = total
-
-    def stem_sum(m, total):
-        return total + dot_t(fx[2 * m : 2 * m + 2].reshape(192, 256), sc_pad[m : m + 2].reshape(64, 256))
-
-    total = jnp.zeros((192, 64), F32)
-    for step in range(33):
-        total = stem_sum(step, total)
+    total = None
+    for k in range(33):
+        term = dot(fx[2 * k : 2 * k + 2].reshape(192, 256), turned(sc_pad[k : k + 2].reshape(64, 256)))
+        total = term if total is None else total + term
     sums_ref[192:384, 64:128] = total
-
     for s in range(SLABS):
         wire_ref[s, 0:SHARE] = sums_ref[s * SHARE : s * SHARE + SHARE, :].astype(BF16)
 

time: 88.9 us -> 87.6 us (0.985)
  Pallas kernels: 9.58 us -> 8.26 us
    pallas_call x1, Pallas kernels: 7.91 us -> 6.59 us  [scenario_pass(): pl.pallas_call(scenario_kernel, out_shape=out_shape, in_specs=[whole] * 1...]
where the time goes in v4:
time: 87.6 us; the launch traced here: 87.2 us
  blocking collectives  37.2 us (42%)
  waiting for transfers between devices  22.1 us (25%)
  starting transfers between devices  12.8 us (15%)
  Pallas kernels  8.26 us (9%)
  local copies, waits for them, and re-layouts  4.54 us (5%)
  other arithmetic  1.41 us (2%)
  between operations  0.95 us (1%)
    all_to_all x2, blocking collectives, exchanged(): return lax.all_to_all(value, axis, split_axis=0, concat_axis=0, tiled=True)  37.2 us
    all_to_all x2, waiting for transfers between devices, exchanged(): return lax.all_to_all(value, axis, split_axis=0, concat_axis=0, tiled=True)  22.1 us
    all_to_all x2, starting transfers between devices, exchanged(): return lax.all_to_all(value, axis, split_axis=0, concat_axis=0, tiled=True)  12.8 us
    pallas_call x1, Pallas kernels, scenario_pass(): pl.pallas_call(scenario_kernel, out_shape=out_shape, in_specs=[whole] * 1...  6.59 us
  transfers between devices with their start and end apart: 2, of which 2 were waited for; matrix products, arithmetic and copies ran while one was open for 7% of the time, Pallas kernels for 0%

profile of v4, /device:TPU:1, one launch (start us, length us, event | category | flops | bytes accessed | tf_op | source)
XLA Modules:
  0.0 87.2 jit_solution(10701974012317094357)
XLA Ops:
  0.6 0.0 copy-start.3
  0.6 0.0 copy-start.4
  0.7 0.0 copy-start.2
  0.7 0.0 copy-start
  0.7 7.1 %all-to-all-start = ((bf16[16,192,256]{2,1,0:T(8,128)(2,1)}), bf16[16,192,256]{2,1,0:T(8,128)(2,1)S(1)}, u32[]{:S(2)}, u32[]{:S(2)}) async-start(bf16[16,192,256]{2,1,0:T(8,128)(2,1)} %bitcast.86), calls=%async_computation | async-start | bytes 3145728 | tf_op jit(solution)/shard_map/all_to_all | solution.py:298
  7.8 0.0 copy-done.3
  7.8 0.1 reshape.74.pc_ref
  7.9 0.0 copy-done.4
  7.9 0.1 copy.56.ow_ref
  8.0 0.0 copy-done.2
  8.0 0.2 copy.45
  8.2 0.1 reshape.64
  8.3 0.0 copy-done
  8.3 0.1 copy.50
  8.5 0.2 copy.52
  8.7 0.1 pad_bitcast_fusion.3
  8.8 0.2 pad_maximum_fusion.2
  9.0 0.0 copy-start.1
  9.0 0.2 reshape.71.w3b_ref
  9.3 0.1 pad_bitcast_fusion.1
  9.3 0.1 pad_maximum_fusion
  9.4 0.2 copy.51
  9.7 0.2 reshape.69.w3_ref
  9.9 0.0 copy-done.1
  10.0 0.1 pad_maximum_fusion.3
  10.0 0.2 copy.60
  10.2 0.2 reshape.80.w2_ref
  10.5 0.1 pad_maximum_fusion.1
  10.6 0.2 copy.46
  10.7 0.4 reshape.65.w1_ref
  11.2 0.1 fusion.17.w2b_ref
  11.3 0.2 select_convert_fusion.3.regroup_ref
  11.5 0.6 select_convert_fusion
  12.1 17.4 %all-to-all-done.x_ref = bf16[16,192,256]{2,1,0:T(8,128)(2,1)S(1)} async-done(((bf16[16,192,256]{2,1,0:T(8,128)(2,1)}), bf16[16,192,256]{2,1,0:T(8,128)(2,1)S(1)}, u32[]{:S(2)}, u32[]{:S(2)}) %all-to-all-start) | async-done | bytes 1572896 | tf_op jit(solution)/shard_map/all_to_all | solution.py:298
  29.5 6.6 %scenario.1 = (f32[16,128]{1,0:T(8,128)S(1)}, bf16[16,168,128]{2,1,0:T(8,128)(2,1)S(1)}) custom-call(bf16[16,192,256]{2,1,0:T(8,128)(2,1)S(1)} %all-to-all-done.x_ref, bf16[128,960]{1,0:T(8,128)(2,1)S(1)} %reshape.65.w1_ref, bf16[128,480]{1,0:T(8,128)(2,1)S(1)} %reshape.80.w2_ref, bf16[128,768]{1,0:T(8,128)(2,1)S(1)} %reshape.69.w3_ref, ...), custom_call_target="tpu_custom_call" | custom-call | flops 4000000000 | bytes 4194304 | tf_op jit(solution)/shard_map/scenario/pallas_call | solution.py:285
  36.1 16.7 %all_to_all.20.got_ref = bf16[16,168,128]{2,1,0:T(8,128)(2,1)S(1)} all-to-all(bf16[16,168,128]{2,1,0:T(8,128)(2,1)S(1)} %get-tuple-element.13), channel_id=1, replica_groups=mesh['lon'=16,'rep'=16] {'lon'}, dimensions={0} | all-to-all | bytes 1376256 | tf_op jit(solution)/shard_map/all_to_all | solution.py:298
  52.8 20.5 %all_to_all.21.got_ref = bf16[16,40,128]{2,1,0:T(8,128)(2,1)S(1)} all-to-all(bf16[16,40,128]{2,1,0:T(8,128)(2,1)S(1)} %lon_share.1), channel_id=1, replica_groups=mesh['lon'=16,'rep'=16] {'rep'}, dimensions={0} | all-to-all | bytes 327680 | tf_op jit(solution)/shard_map/all_to_all | solution.py:298
  73.3 0.7 rep_share.1
  74.0 5.8 %all-to-all-start.3 = ((bf16[16,40,128]{2,1,0:T(8,128)(2,1)}), bf16[16,40,128]{2,1,0:T(8,128)(2,1)S(1)}, u32[]{:S(2)}, u32[]{:S(2)}) async-start(bf16[16,40,128]{2,1,0:T(8,128)(2,1)} %rep_share.1), calls=%async_computation.3 | async-start | bytes 327680 | tf_op jit(solution)/shard_map/all_to_all | solution.py:298
  79.8 0.1 reshape.75
  79.9 0.6 copy.57
  80.5 1.1 %copy.64 = bf16[16,4,32,128]{3,1,2,0:T(4,128)(2,1)} copy(bf16[16,4,32,128]{3,2,1,0:T(8,128)(2,1)S(1)} %bitcast.85) | data formatting | bytes 1048576 | tf_op jit(solution)/shard_map/reshape | solution.py:367
  81.6 4.7 %all-to-all-done.3 = bf16[16,40,128]{2,1,0:T(8,128)(2,1)S(1)} async-done(((bf16[16,40,128]{2,1,0:T(8,128)(2,1)}), bf16[16,40,128]{2,1,0:T(8,128)(2,1)S(1)}, u32[]{:S(2)}, u32[]{:S(2)}) %all-to-all-start.3) | async-done | bytes 163872 | tf_op jit(solution)/shard_map/all_to_all | solution.py:298
  86.3 0.9 %unpack.1 = (f32[24,4,4,32]{3,2,1,0:T(4,128)}, f32[3,3,32,64]{3,2,1,0:T(8,128)}, f32[3,3,64,64]{3,2,1,0:T(8,128)}, f32[1,64]{1,0:T(1,128)}) custom-call(bf16[640,128]{1,0:T(8,128)(2,1)S(1)} %bitcast.84), custom_call_target="tpu_custom_call" | custom-call | tf_op jit(solution)/shard_map/unpack/pallas_call | solution.py:333
  (20 shorter events, 0.3 us)
Async XLA Ops:
  0.6 7.2 %copy-start.3 = (f32[1,32,64]{2,1,0:T(8,128)S(1)}, f32[1,32,64]{2,1,0:T(8,128)}, u32[]{:S(2)}) copy-start(f32[1,32,64]{2,1,0:T(8,128)} %param.11) | copy-start | bytes 24580
  0.6 7.3 %copy-start.4 = (f32[64]{0:T(128)S(1)}, f32[64]{0:T(128)}, u32[]{:S(2)}) copy-start(f32[64]{0:T(128)} %param.10) | copy-start | bytes 772
  0.7 7.4 %copy-start.2 = (bf16[32,24,4,4]{0,3,2,1:T(4,128)(2,1)S(1)}, bf16[32,24,4,4]{0,3,2,1:T(4,128)(2,1)}, u32[]{:S(2)}) copy-start(bf16[32,24,4,4]{0,3,2,1:T(4,128)(2,1)} %param.7) | copy-start | bytes 73732
  0.7 7.7 %copy-start = (bf16[64,64,3,3]{1,0,3,2:T(8,128)(2,1)S(1)}, bf16[64,64,3,3]{1,0,3,2:T(8,128)(2,1)}, u32[]{:S(2)}) copy-start(bf16[64,64,3,3]{1,0,3,2:T(8,128)(2,1)} %param.9) | copy-start | bytes 221188
  0.7 28.9 %all-to-all-start = ((bf16[16,192,256]{2,1,0:T(8,128)(2,1)}), bf16[16,192,256]{2,1,0:T(8,128)(2,1)S(1)}, u32[]{:S(2)}, u32[]{:S(2)}) async-start(bf16[16,192,256]{2,1,0:T(8,128)(2,1)} %bitcast.86), calls=%async_computation | async-start | bytes 3145728 | tf_op jit(solution)/shard_map/all_to_all | solution.py:298
  9.0 0.9 %copy-start.1 = (bf16[64,32,3,3]{0,1,3,2:T(8,128)(2,1)S(1)}, bf16[64,32,3,3]{0,1,3,2:T(8,128)(2,1)}, u32[]{:S(2)}) copy-start(bf16[64,32,3,3]{0,1,3,2:T(8,128)(2,1)} %param.8) | copy-start | bytes 110596
  74.0 12.3 %all-to-all-start.3 = ((bf16[16,40,128]{2,1,0:T(8,128)(2,1)}), bf16[16,40,128]{2,1,0:T(8,128)(2,1)S(1)}, u32[]{:S(2)}, u32[]{:S(2)}) async-start(bf16[16,40,128]{2,1,0:T(8,128)(2,1)} %rep_share.1), calls=%async_computation.3 | async-start | bytes 327680 | tf_op jit(solution)/shard_map/all_to_all | solution.py:298

commit v5 on v4

--- a/solution.py
+++ b/solution.py
@@ -294,21 +294,24 @@
     )(x, *weights, *selections(), out_weight.reshape(C2, 1), cotangent)
 
 
-def exchanged(value, axis):
-    return lax.all_to_all(value, axis, split_axis=0, concat_axis=0, tiled=True)
+def exchanged(value, axis, groups=None):
+    return lax.all_to_all(
+        value, axis, split_axis=0, concat_axis=0, tiled=True, axis_index_groups=groups
+    )
 
 
 def share_kernel(got_ref, out_ref):
     total = jnp.zeros((SHARE, 128), F32)
-    for k in range(SLABS):
+    for k in range(got_ref.shape[0]):
         total = total + got_ref[k, 0:SHARE].astype(F32)
     share = total.astype(BF16)
-    for k in range(SLABS):
+    for k in range(out_ref.shape[0]):
         out_ref[k] = share
 
 
 def unpack_kernel(factor, sums_ref, stem_ref, mid_ref, head_ref, out_ref, wide):
-    wide[...] = sums_ref[...].astype(F32) * factor
+    rows = SLABS * SHARE
+    wide[...] = (sums_ref[0:rows].astype(F32) + sums_ref[rows : 2 * rows].astype(F32)) * factor
     for a in range(3):
         at = (2 - a) * C2
         head_ref[a, 0] = wide[at : at + C2, 0:64]
@@ -321,10 +324,11 @@
     for a in range(4):
         lanes = slice(64, 96) if a >= 2 else slice(96, 128)
         for c in range(CIN):
-            rows = wide[pl.ds(192 + a % 2 * 96 + c, 4, stride=CIN), :]
-            stem_ref[c, a] = rows[:, lanes]
+            taps = wide[pl.ds(192 + a % 2 * 96 + c, 4, stride=CIN), :]
+            stem_ref[c, a] = taps[:, lanes]
     ones = jnp.full((8, 128), 1.0, BF16)
-    out_ref[...] = dot_t(ones, sums_ref[576:640])[0:1] * factor
+    out_sums = [dot_t(ones, sums_ref[at + 576 : at + 640])[0:1] for at in (0, rows)]
+    out_ref[...] = (out_sums[0] + out_sums[1]) * factor
 
 
 def on_chip(kernel, outs, scratch=(), name=None):
@@ -342,10 +346,16 @@
 
 
 def summed_everywhere(got, factor):
-    shares = jax.ShapeDtypeStruct((SLABS, SHARE, 128), BF16)
-    share = on_chip(share_kernel, shares, name="lon_share")(got)
-    share = on_chip(share_kernel, shares, name="rep_share")(exchanged(share, "rep"))
-    sums = exchanged(share, "lon").reshape(SLABS * SHARE, 128)
+    lon, rep = lax.axis_size("lon"), lax.axis_size("rep")
+    lines = [list(range(parity, rep, 2)) for parity in (0, 1)]
+    planes = [
+        [(2 * z + parity) * lon + k for parity in (0, 1) for k in range(lon)] for z in range(rep // 2)
+    ]
+    one_line = jax.ShapeDtypeStruct((rep // 2, SHARE, 128), BF16)
+    one_plane = jax.ShapeDtypeStruct((2 * lon, SHARE, 128), BF16)
+    share = on_chip(share_kernel, one_line, name="lon_share")(got)
+    share = on_chip(share_kernel, one_plane, name="line_share")(exchanged(share, "rep", lines))
+    sums = exchanged(share, ("rep", "lon"), planes).reshape(2 * SLABS * SHARE, 128)
     outs = (
         jax.ShapeDtypeStruct((CIN, 4, 4, C1), F32),
         jax.ShapeDtypeStruct((3, 3, C1, C2), F32),

time: 87.6 us -> 86.6 us (0.989)
  blocking collectives: 37.2 us -> 32.2 us
  waiting for transfers between devices: 22.1 us -> 25.2 us
  starting transfers between devices: 12.8 us -> 13.7 us
    all_to_all x2, blocking collectives: 37.2 us -> 32.2 us  [exchanged(): lax.all_to_all(value, axis, split_axis=0, concat_axis=0, tiled=True, axis...]
    all_to_all x2, waiting for transfers between devices: 22.1 us -> 25.2 us  [exchanged(): lax.all_to_all(value, axis, split_axis=0, concat_axis=0, tiled=True, axis...]
where the time goes in v5:
time: 86.6 us; the launch traced here: 86.3 us
  blocking collectives  32.2 us (37%)
  waiting for transfers between devices  25.2 us (29%)
  starting transfers between devices  13.7 us (16%)
  Pallas kernels  8.33 us (10%)
  local copies, waits for them, and re-layouts  4.54 us (5%)
  other arithmetic  1.41 us (2%)
  between operations  0.96 us (1%)
    all_to_all x2, blocking collectives, exchanged(): lax.all_to_all(value, axis, split_axis=0, concat_axis=0, tiled=True, axis...  32.2 us
    all_to_all x2, waiting for transfers between devices, exchanged(): lax.all_to_all(value, axis, split_axis=0, concat_axis=0, tiled=True, axis...  25.2 us
    all_to_all x2, starting transfers between devices, exchanged(): lax.all_to_all(value, axis, split_axis=0, concat_axis=0, tiled=True, axis...  13.7 us
    pallas_call x1, Pallas kernels, scenario_pass(): pl.pallas_call(scenario_kernel, out_shape=out_shape, in_specs=[whole] * 1...  6.59 us
    pallas_call x3, Pallas kernels, on_chip(): pl.pallas_call(kernel, out_shape=outs, in_specs=[whole] * len(args), out_...  1.74 us
  transfers between devices with their start and end apart: 2, of which 2 were waited for; matrix products, arithmetic and copies ran while one was open for 7% of the time, Pallas kernels for 0%

profile of v5, /device:TPU:1, one launch (start us, length us, event | category | flops | bytes accessed | tf_op | source)
XLA Modules:
  0.0 86.3 jit_solution(10509078622023361977)
XLA Ops:
  0.6 0.0 copy-start.3
  0.6 0.0 copy-start.4
  0.7 0.0 copy-start.2
  0.7 0.0 copy-start
  0.7 7.1 %all-to-all-start = ((bf16[16,192,256]{2,1,0:T(8,128)(2,1)}), bf16[16,192,256]{2,1,0:T(8,128)(2,1)S(1)}, u32[]{:S(2)}, u32[]{:S(2)}) async-start(bf16[16,192,256]{2,1,0:T(8,128)(2,1)} %bitcast.86), calls=%async_computation | async-start | bytes 3145728 | tf_op jit(solution)/shard_map/all_to_all | solution.py:298
  7.8 0.0 copy-done.3
  7.8 0.1 reshape.74.pc_ref
  7.9 0.0 copy-done.4
  7.9 0.1 copy.56.ow_ref
  8.0 0.0 copy-done.2
  8.0 0.2 copy.45
  8.2 0.1 reshape.64
  8.3 0.0 copy-done
  8.3 0.1 copy.50
  8.5 0.2 copy.52
  8.7 0.1 pad_bitcast_fusion.3
  8.8 0.2 pad_maximum_fusion.2
  9.0 0.0 copy-start.1
  9.0 0.2 reshape.71.w3b_ref
  9.3 0.1 pad_bitcast_fusion.1
  9.3 0.1 pad_maximum_fusion
  9.4 0.2 copy.51
  9.7 0.2 reshape.69.w3_ref
  9.9 0.0 copy-done.1
  10.0 0.1 pad_maximum_fusion.3
  10.0 0.2 copy.60
  10.2 0.2 reshape.80.w2_ref
  10.5 0.1 pad_maximum_fusion.1
  10.6 0.2 copy.46
  10.7 0.4 reshape.65.w1_ref
  11.2 0.1 fusion.17.w2b_ref
  11.3 0.2 select_convert_fusion.3.regroup_ref
  11.5 0.6 select_convert_fusion
  12.1 17.4 %all-to-all-done.x_ref = bf16[16,192,256]{2,1,0:T(8,128)(2,1)S(1)} async-done(((bf16[16,192,256]{2,1,0:T(8,128)(2,1)}), bf16[16,192,256]{2,1,0:T(8,128)(2,1)S(1)}, u32[]{:S(2)}, u32[]{:S(2)}) %all-to-all-start) | async-done | bytes 1572896 | tf_op jit(solution)/shard_map/all_to_all | solution.py:298
  29.5 6.6 %scenario.1 = (f32[16,128]{1,0:T(8,128)S(1)}, bf16[16,168,128]{2,1,0:T(8,128)(2,1)S(1)}) custom-call(bf16[16,192,256]{2,1,0:T(8,128)(2,1)S(1)} %all-to-all-done.x_ref, bf16[128,960]{1,0:T(8,128)(2,1)S(1)} %reshape.65.w1_ref, bf16[128,480]{1,0:T(8,128)(2,1)S(1)} %reshape.80.w2_ref, bf16[128,768]{1,0:T(8,128)(2,1)S(1)} %reshape.69.w3_ref, ...), custom_call_target="tpu_custom_call" | custom-call | flops 4000000000 | bytes 4194304 | tf_op jit(solution)/shard_map/scenario/pallas_call | solution.py:285
  36.1 16.7 %all_to_all.20.got_ref = bf16[16,168,128]{2,1,0:T(8,128)(2,1)S(1)} all-to-all(bf16[16,168,128]{2,1,0:T(8,128)(2,1)S(1)} %get-tuple-element.13), channel_id=1, replica_groups=mesh['lon'=16,'rep'=16] {'lon'}, dimensions={0} | all-to-all | bytes 1376256 | tf_op jit(solution)/shard_map/all_to_all | solution.py:298
  52.8 15.5 %all_to_all.21.got_ref = bf16[8,40,128]{2,1,0:T(8,128)(2,1)S(1)} all-to-all(bf16[8,40,128]{2,1,0:T(8,128)(2,1)S(1)} %lon_share.1), channel_id=1, replica_groups={{0,2,4,6,8,10,12,14},{1,3,5,7,9,11,13,15},{16,18,20,22,24,26,28,30},{17..., dimensions={0} | all-to-all | bytes 163840 | tf_op jit(solution)/shard_map/all_to_all | solution.py:298
  68.3 0.8 line_share.1
  69.1 6.6 %all-to-all-start.3 = ((bf16[32,40,128]{2,1,0:T(8,128)(2,1)}), bf16[32,40,128]{2,1,0:T(8,128)(2,1)S(1)}, u32[]{:S(2)}, u32[]{:S(2)}) async-start(bf16[32,40,128]{2,1,0:T(8,128)(2,1)} %line_share.1), calls=%async_computation.3 | async-start | bytes 655360 | tf_op jit(solution)/shard_map/all_to_all | solution.py:298
  75.7 0.1 reshape.75
  75.8 0.6 copy.57
  76.4 1.1 %copy.64 = bf16[16,4,32,128]{3,1,2,0:T(4,128)(2,1)} copy(bf16[16,4,32,128]{3,2,1,0:T(8,128)(2,1)S(1)} %bitcast.85) | data formatting | bytes 1048576 | tf_op jit(solution)/shard_map/reshape | solution.py:377
  77.5 7.8 %all-to-all-done.3 = bf16[32,40,128]{2,1,0:T(8,128)(2,1)S(1)} async-done(((bf16[32,40,128]{2,1,0:T(8,128)(2,1)}), bf16[32,40,128]{2,1,0:T(8,128)(2,1)S(1)}, u32[]{:S(2)}, u32[]{:S(2)}) %all-to-all-start.3) | async-done | bytes 327712 | tf_op jit(solution)/shard_map/all_to_all | solution.py:298
  85.3 0.9 %unpack.1 = (f32[24,4,4,32]{3,2,1,0:T(4,128)}, f32[3,3,32,64]{3,2,1,0:T(8,128)}, f32[3,3,64,64]{3,2,1,0:T(8,128)}, f32[1,64]{1,0:T(1,128)}) custom-call(bf16[1280,128]{1,0:T(8,128)(2,1)S(1)} %bitcast.84), custom_call_target="tpu_custom_call" | custom-call | tf_op jit(solution)/shard_map/unpack/pallas_call | solution.py:337
  (20 shorter events, 0.3 us)
Async XLA Ops:
  0.6 7.2 %copy-start.3 = (f32[1,32,64]{2,1,0:T(8,128)S(1)}, f32[1,32,64]{2,1,0:T(8,128)}, u32[]{:S(2)}) copy-start(f32[1,32,64]{2,1,0:T(8,128)} %param.11) | copy-start | bytes 24580
  0.6 7.3 %copy-start.4 = (f32[64]{0:T(128)S(1)}, f32[64]{0:T(128)}, u32[]{:S(2)}) copy-start(f32[64]{0:T(128)} %param.10) | copy-start | bytes 772
  0.7 7.4 %copy-start.2 = (bf16[32,24,4,4]{0,3,2,1:T(4,128)(2,1)S(1)}, bf16[32,24,4,4]{0,3,2,1:T(4,128)(2,1)}, u32[]{:S(2)}) copy-start(bf16[32,24,4,4]{0,3,2,1:T(4,128)(2,1)} %param.7) | copy-start | bytes 73732
  0.7 7.7 %copy-start = (bf16[64,64,3,3]{1,0,3,2:T(8,128)(2,1)S(1)}, bf16[64,64,3,3]{1,0,3,2:T(8,128)(2,1)}, u32[]{:S(2)}) copy-start(bf16[64,64,3,3]{1,0,3,2:T(8,128)(2,1)} %param.9) | copy-start | bytes 221188
  0.7 28.9 %all-to-all-start = ((bf16[16,192,256]{2,1,0:T(8,128)(2,1)}), bf16[16,192,256]{2,1,0:T(8,128)(2,1)S(1)}, u32[]{:S(2)}, u32[]{:S(2)}) async-start(bf16[16,192,256]{2,1,0:T(8,128)(2,1)} %bitcast.86), calls=%async_computation | async-start | bytes 3145728 | tf_op jit(solution)/shard_map/all_to_all | solution.py:298
  9.0 0.9 %copy-start.1 = (bf16[64,32,3,3]{0,1,3,2:T(8,128)(2,1)S(1)}, bf16[64,32,3,3]{0,1,3,2:T(8,128)(2,1)}, u32[]{:S(2)}) copy-start(bf16[64,32,3,3]{0,1,3,2:T(8,128)(2,1)} %param.8) | copy-start | bytes 110596
  69.1 16.2 %all-to-all-start.3 = ((bf16[32,40,128]{2,1,0:T(8,128)(2,1)}), bf16[32,40,128]{2,1,0:T(8,128)(2,1)S(1)}, u32[]{:S(2)}, u32[]{:S(2)}) async-start(bf16[32,40,128]{2,1,0:T(8,128)(2,1)} %line_share.1), calls=%async_computation.3 | async-start | bytes 655360 | tf_op jit(solution)/shard_map/all_to_all | solution.py:298

commit v6 on v5

--- a/solution.py
+++ b/solution.py
@@ -85,6 +85,14 @@
     return lax.dot_general(left, right, (((1,), (1,)), ((), ())), preferred_element_type=F32)
 
 
+def side_by_side(weights, windows):
+    out = []
+    for at in range(0, len(windows), 2):
+        both = dot(weights, jnp.concatenate(windows[at : at + 2], 1))
+        out += [both[:, 0:128], both[:, 128:256]]
+    return out
+
+
 def turned(block):
     return block.astype(F32).T.astype(BF16)
 
@@ -160,18 +168,22 @@
     mx[0] = swapped(mx[32])
     mx[33] = jnp.zeros((96, 128), BF16)
 
-    def mid(g):
+    def mid_window(g):
         n = MID_GROUP
-        window = mx[pl.ds(2 * n * g, 2 * n + 1)].reshape((2 * n + 1) * 96, 128)
-        pre = dot(w2_ref[...], window)
+        return mx[2 * n * g : 2 * n * g + 2 * n + 1].reshape((2 * n + 1) * 96, 128)
+
+    def mid(g, pre):
+        n = MID_GROUP
         mid_pre[n * g : n * g + n] = pre.reshape(n, C2, 128)
         act = pre * sigmoid(pre)
         for k in range(n):
             one = act[k * C2 : k * C2 + C2]
             hx[n * g + k + 1] = jnp.concatenate([earlier(one), one, later(one)], 0).astype(BF16)
 
-    for step in range(16 // MID_GROUP):
-        mid(step)
+    for step in range(0, 16 // MID_GROUP, 2):
+        pres = side_by_side(w2_ref[...], [mid_window(step), mid_window(step + 1)])
+        mid(step, pres[0])
+        mid(step + 1, pres[1])
     hx[0] = swapped(hx[16])
     hx[17] = swapped(hx[1])
 
@@ -179,10 +191,12 @@
         hc_pad[edge] = jnp.zeros((C2, 128), BF16)
     out_w = jnp.broadcast_to(ow_ref[...], (C2, 128))
 
-    def head(g, out_sum):
+    def head_window(maps, g):
         n = HEAD_GROUP
-        window = hx[pl.ds(n * g, n + 2)].reshape((n + 2) * 192, 128)
-        pre = dot(w3_ref[...], window)
+        return maps[n * g : n * g + n + 2].reshape((n + 2) * 192, 128)
+
+    def head(g, pre, out_sum):
+        n = HEAD_GROUP
         sigma = sigmoid(pre)
         act = (pre * sigma).astype(BF16).astype(F32)
         bend = sigma * (1.0 + pre * (1.0 - sigma))
@@ -198,8 +212,10 @@
         return out_sum
 
     out_sum = jnp.zeros((C2, 128), F32)
-    for step in range(16 // HEAD_GROUP):
-        out_sum = head(step, out_sum)
+    for step in range(0, 16 // HEAD_GROUP, 2):
+        pres = side_by_side(w3_ref[...], [head_window(hx, step), head_window(hx, step + 1)])
+        out_sum = head(step, pres[0], out_sum)
+        out_sum = head(step + 1, pres[1], out_sum)
     sums_ref[576:640, :] = out_sum
     hc_wide[0] = swapped(hc_wide[16])
     hc_wide[17] = swapped(hc_wide[1])
@@ -207,18 +223,19 @@
     for edge in (0, 17):
         mc_pad[edge] = jnp.zeros((C2, 128), BF16)
 
-    def head_back(g):
+    def head_back(g, grad):
         n = HEAD_GROUP
-        window = hc_wide[pl.ds(n * g, n + 2)].reshape((n + 2) * 192, 128)
-        grad = dot(w3b_ref[...], window).astype(BF16).astype(F32)
+        grad = grad.astype(BF16).astype(F32)
         mc = grad * slope_of(mid_pre[n * g : n * g + n].reshape(n * C2, 128))
         for k in range(n):
             one = mc[k * C2 : k * C2 + C2]
             mc_pad[n * g + k + 1] = one.astype(BF16)
             mc_pair[n * g + k] = jnp.concatenate([one, later(one)], 0).astype(BF16)
 
-    for step in range(16 // HEAD_GROUP):
-        head_back(step)
+    for step in range(0, 16 // HEAD_GROUP, 2):
+        grads = side_by_side(w3b_ref[...], [head_window(hc_wide, step), head_window(hc_wide, step + 1)])
+        head_back(step, grads[0])
+        head_back(step + 1, grads[1])
     mc_pair[16] = swapped(mc_pair[0])
 
     for edge in (0, 33):
@@ -226,9 +243,9 @@
 
     def mid_back(at):
         parts = []
-        for r in range(at, at + BACK_BATCH):
-            window = mc_pair[r : r + 2].reshape(256, 128)
-            grad = dot(w2b_ref[...], window).astype(BF16)
+        windows = [mc_pair[r : r + 2].reshape(256, 128) for r in range(at, at + BACK_BATCH)]
+        for grad in side_by_side(w2b_ref[...], windows):
+            grad = grad.astype(BF16)
             parts.append(jnp.concatenate([grad[0:64], grad[64:128]], 1))
         grads = dot(jnp.concatenate(parts, 0), inter_ref[...])
         for m in range(at // 2, (at + BACK_BATCH) // 2):

time: 86.6 us -> 86.3 us (level)
  no operation moved by 1% of the time
where the time goes in v6:
time: 86.3 us; the launch traced here: 85.9 us
  blocking collectives  32.1 us (37%)
  waiting for transfers between devices  25.2 us (29%)
  starting transfers between devices  13.7 us (16%)
  Pallas kernels  7.97 us (9%)
  local copies, waits for them, and re-layouts  4.54 us (5%)
  other arithmetic  1.41 us (2%)
  between operations  0.96 us (1%)
    all_to_all x2, blocking collectives, exchanged(): lax.all_to_all(value, axis, split_axis=0, concat_axis=0, tiled=True, axis...  32.1 us
    all_to_all x2, waiting for transfers between devices, exchanged(): lax.all_to_all(value, axis, split_axis=0, concat_axis=0, tiled=True, axis...  25.2 us
    all_to_all x2, starting transfers between devices, exchanged(): lax.all_to_all(value, axis, split_axis=0, concat_axis=0, tiled=True, axis...  13.7 us
    pallas_call x1, Pallas kernels, scenario_pass(): pl.pallas_call(scenario_kernel, out_shape=out_shape, in_specs=[whole] * 1...  6.23 us
    pallas_call x3, Pallas kernels, on_chip(): pl.pallas_call(kernel, out_shape=outs, in_specs=[whole] * len(args), out_...  1.74 us
  transfers between devices with their start and end apart: 2, of which 2 were waited for; matrix products, arithmetic and copies ran while one was open for 7% of the time, Pallas kernels for 0%

profile of v6, /device:TPU:1, one launch (start us, length us, event | category | flops | bytes accessed | tf_op | source)
XLA Modules:
  0.0 85.9 jit_solution(9378053163480914976)
XLA Ops:
  0.6 0.0 copy-start.3
  0.6 0.0 copy-start.4
  0.7 0.0 copy-start.2
  0.7 0.0 copy-start
  0.7 7.1 %all-to-all-start = ((bf16[16,192,256]{2,1,0:T(8,128)(2,1)}), bf16[16,192,256]{2,1,0:T(8,128)(2,1)S(1)}, u32[]{:S(2)}, u32[]{:S(2)}) async-start(bf16[16,192,256]{2,1,0:T(8,128)(2,1)} %bitcast.86), calls=%async_computation | async-start | bytes 3145728 | tf_op jit(solution)/shard_map/all_to_all | solution.py:315
  7.8 0.0 copy-done.3
  7.8 0.1 reshape.74.pc_ref
  7.9 0.0 copy-done.4
  7.9 0.1 copy.56.ow_ref
  8.0 0.0 copy-done.2
  8.0 0.2 copy.45
  8.2 0.1 reshape.64
  8.3 0.0 copy-done
  8.3 0.1 copy.50
  8.5 0.2 copy.52
  8.7 0.1 pad_bitcast_fusion.3
  8.8 0.2 pad_maximum_fusion.2
  9.0 0.0 copy-start.1
  9.0 0.2 reshape.71.w3b_ref
  9.3 0.1 pad_bitcast_fusion.1
  9.3 0.1 pad_maximum_fusion
  9.4 0.2 copy.51
  9.7 0.2 reshape.69.w3_ref
  9.9 0.0 copy-done.1
  10.0 0.1 pad_maximum_fusion.3
  10.0 0.2 copy.60
  10.2 0.2 reshape.80.w2_ref
  10.5 0.1 pad_maximum_fusion.1
  10.6 0.2 copy.46
  10.7 0.4 reshape.65.w1_ref
  11.2 0.1 fusion.17.w2b_ref
  11.3 0.2 select_convert_fusion.3.regroup_ref
  11.5 0.6 select_convert_fusion
  12.1 17.4 %all-to-all-done.x_ref = bf16[16,192,256]{2,1,0:T(8,128)(2,1)S(1)} async-done(((bf16[16,192,256]{2,1,0:T(8,128)(2,1)}), bf16[16,192,256]{2,1,0:T(8,128)(2,1)S(1)}, u32[]{:S(2)}, u32[]{:S(2)}) %all-to-all-start) | async-done | bytes 1572896 | tf_op jit(solution)/shard_map/all_to_all | solution.py:315
  29.5 6.2 %scenario.1 = (f32[16,128]{1,0:T(8,128)S(1)}, bf16[16,168,128]{2,1,0:T(8,128)(2,1)S(1)}) custom-call(bf16[16,192,256]{2,1,0:T(8,128)(2,1)S(1)} %all-to-all-done.x_ref, bf16[128,960]{1,0:T(8,128)(2,1)S(1)} %reshape.65.w1_ref, bf16[128,480]{1,0:T(8,128)(2,1)S(1)} %reshape.80.w2_ref, bf16[128,768]{1,0:T(8,128)(2,1)S(1)} %reshape.69.w3_ref, ...), custom_call_target="tpu_custom_call" | custom-call | flops 4000000000 | bytes 4194304 | tf_op jit(solution)/shard_map/scenario/pallas_call | solution.py:302
  35.8 16.6 %all_to_all.20.got_ref = bf16[16,168,128]{2,1,0:T(8,128)(2,1)S(1)} all-to-all(bf16[16,168,128]{2,1,0:T(8,128)(2,1)S(1)} %get-tuple-element.13), channel_id=1, replica_groups=mesh['lon'=16,'rep'=16] {'lon'}, dimensions={0} | all-to-all | bytes 1376256 | tf_op jit(solution)/shard_map/all_to_all | solution.py:315
  52.4 15.5 %all_to_all.21.got_ref = bf16[8,40,128]{2,1,0:T(8,128)(2,1)S(1)} all-to-all(bf16[8,40,128]{2,1,0:T(8,128)(2,1)S(1)} %lon_share.1), channel_id=1, replica_groups={{0,2,4,6,8,10,12,14},{1,3,5,7,9,11,13,15},{16,18,20,22,24,26,28,30},{17..., dimensions={0} | all-to-all | bytes 163840 | tf_op jit(solution)/shard_map/all_to_all | solution.py:315
  67.9 0.8 line_share.1
  68.7 6.6 %all-to-all-start.3 = ((bf16[32,40,128]{2,1,0:T(8,128)(2,1)}), bf16[32,40,128]{2,1,0:T(8,128)(2,1)S(1)}, u32[]{:S(2)}, u32[]{:S(2)}) async-start(bf16[32,40,128]{2,1,0:T(8,128)(2,1)} %line_share.1), calls=%async_computation.3 | async-start | bytes 655360 | tf_op jit(solution)/shard_map/all_to_all | solution.py:315
  75.3 0.1 reshape.75
  75.4 0.6 copy.57
  76.1 1.1 %copy.64 = bf16[16,4,32,128]{3,1,2,0:T(4,128)(2,1)} copy(bf16[16,4,32,128]{3,2,1,0:T(8,128)(2,1)S(1)} %bitcast.85) | data formatting | bytes 1048576 | tf_op jit(solution)/shard_map/reshape | solution.py:394
  77.1 7.8 %all-to-all-done.3 = bf16[32,40,128]{2,1,0:T(8,128)(2,1)S(1)} async-done(((bf16[32,40,128]{2,1,0:T(8,128)(2,1)}), bf16[32,40,128]{2,1,0:T(8,128)(2,1)S(1)}, u32[]{:S(2)}, u32[]{:S(2)}) %all-to-all-start.3) | async-done | bytes 327712 | tf_op jit(solution)/shard_map/all_to_all | solution.py:315
  85.0 0.9 %unpack.1 = (f32[24,4,4,32]{3,2,1,0:T(4,128)}, f32[3,3,32,64]{3,2,1,0:T(8,128)}, f32[3,3,64,64]{3,2,1,0:T(8,128)}, f32[1,64]{1,0:T(1,128)}) custom-call(bf16[1280,128]{1,0:T(8,128)(2,1)S(1)} %bitcast.84), custom_call_target="tpu_custom_call" | custom-call | tf_op jit(solution)/shard_map/unpack/pallas_call | solution.py:354
  (20 shorter events, 0.3 us)
Async XLA Ops:
  0.6 7.2 %copy-start.3 = (f32[1,32,64]{2,1,0:T(8,128)S(1)}, f32[1,32,64]{2,1,0:T(8,128)}, u32[]{:S(2)}) copy-start(f32[1,32,64]{2,1,0:T(8,128)} %param.11) | copy-start | bytes 24580
  0.6 7.3 %copy-start.4 = (f32[64]{0:T(128)S(1)}, f32[64]{0:T(128)}, u32[]{:S(2)}) copy-start(f32[64]{0:T(128)} %param.10) | copy-start | bytes 772
  0.7 7.4 %copy-start.2 = (bf16[32,24,4,4]{0,3,2,1:T(4,128)(2,1)S(1)}, bf16[32,24,4,4]{0,3,2,1:T(4,128)(2,1)}, u32[]{:S(2)}) copy-start(bf16[32,24,4,4]{0,3,2,1:T(4,128)(2,1)} %param.7) | copy-start | bytes 73732
  0.7 7.7 %copy-start = (bf16[64,64,3,3]{1,0,3,2:T(8,128)(2,1)S(1)}, bf16[64,64,3,3]{1,0,3,2:T(8,128)(2,1)}, u32[]{:S(2)}) copy-start(bf16[64,64,3,3]{1,0,3,2:T(8,128)(2,1)} %param.9) | copy-start | bytes 221188
  0.7 28.9 %all-to-all-start = ((bf16[16,192,256]{2,1,0:T(8,128)(2,1)}), bf16[16,192,256]{2,1,0:T(8,128)(2,1)S(1)}, u32[]{:S(2)}, u32[]{:S(2)}) async-start(bf16[16,192,256]{2,1,0:T(8,128)(2,1)} %bitcast.86), calls=%async_computation | async-start | bytes 3145728 | tf_op jit(solution)/shard_map/all_to_all | solution.py:315
  9.0 0.9 %copy-start.1 = (bf16[64,32,3,3]{0,1,3,2:T(8,128)(2,1)S(1)}, bf16[64,32,3,3]{0,1,3,2:T(8,128)(2,1)}, u32[]{:S(2)}) copy-start(bf16[64,32,3,3]{0,1,3,2:T(8,128)(2,1)} %param.8) | copy-start | bytes 110596
  68.7 16.3 %all-to-all-start.3 = ((bf16[32,40,128]{2,1,0:T(8,128)(2,1)}), bf16[32,40,128]{2,1,0:T(8,128)(2,1)S(1)}, u32[]{:S(2)}, u32[]{:S(2)}) async-start(bf16[32,40,128]{2,1,0:T(8,128)(2,1)} %line_share.1), calls=%async_computation.3 | async-start | bytes 655360 | tf_op jit(solution)/shard_map/all_to_all | solution.py:315

commit v7 on v6

--- a/solution.py
+++ b/solution.py
@@ -12,7 +12,7 @@
 C1, C2 = 32, 64
 COT_ROWS, SHARE = 128, 40
 WIRE_ROWS = SHARE + COT_ROWS
-STEM_GROUP, STEM_BATCH, MID_GROUP, HEAD_GROUP = 4, 4, 2, 2
+STEM_GROUP, STEM_BATCH, MID_GROUP, HEAD_GROUP = 4, 4, 1, 1
 SLAB_BATCH, BACK_BATCH = 2, 8
 
 

time: 86.3 us -> 86.2 us (level)
  waiting for transfers between devices: 25.2 us -> 26.7 us
  local copies, waits for them, and re-layouts: 4.54 us -> 3.45 us
    all_to_all x2, waiting for transfers between devices: 25.2 us -> 26.7 us  [exchanged(): lax.all_to_all(value, axis, split_axis=0, concat_axis=0, tiled=True, axis...]
  transfers between devices with their start and end apart: 2 -> 2, of which waited for: 2 -> 2; matrix products, arithmetic and copies ran while one was open for 7% -> 5% of each run, Pallas kernels for 0% -> 0%
where the time goes in v7:
time: 86.2 us; the launch traced here: 85.9 us
  blocking collectives  32.1 us (37%)
  waiting for transfers between devices  26.7 us (31%)
  starting transfers between devices  13.7 us (16%)
  Pallas kernels  7.91 us (9%)
  local copies, waits for them, and re-layouts  3.45 us (4%)
  other arithmetic  1.06 us (1%)
  between operations  0.89 us (1%)
    all_to_all x2, blocking collectives, exchanged(): lax.all_to_all(value, axis, split_axis=0, concat_axis=0, tiled=True, axis...  32.1 us
    all_to_all x2, waiting for transfers between devices, exchanged(): lax.all_to_all(value, axis, split_axis=0, concat_axis=0, tiled=True, axis...  26.7 us
    all_to_all x2, starting transfers between devices, exchanged(): lax.all_to_all(value, axis, split_axis=0, concat_axis=0, tiled=True, axis...  13.7 us
    pallas_call x1, Pallas kernels, scenario_pass(): pl.pallas_call(scenario_kernel, out_shape=out_shape, in_specs=[whole] * 1...  6.19 us
  transfers between devices with their start and end apart: 2, of which 2 were waited for; matrix products, arithmetic and copies ran while one was open for 5% of the time, Pallas kernels for 0%

profile of v7, /device:TPU:1, one launch (start us, length us, event | category | flops | bytes accessed | tf_op | source)
XLA Modules:
  0.0 85.9 jit_solution(11638126329167898717)
XLA Ops:
  0.6 0.0 copy-start.3
  0.6 0.0 copy-start.4
  0.7 0.0 copy-start.1
  0.7 0.0 copy-start.2
  0.7 0.0 copy-start
  0.7 7.1 %all-to-all-start = ((bf16[16,192,256]{2,1,0:T(8,128)(2,1)}), bf16[16,192,256]{2,1,0:T(8,128)(2,1)S(1)}, u32[]{:S(2)}, u32[]{:S(2)}) async-start(bf16[16,192,256]{2,1,0:T(8,128)(2,1)} %bitcast.74), calls=%async_computation | async-start | bytes 3145728 | tf_op jit(solution)/shard_map/all_to_all | solution.py:315
  7.8 0.0 copy-done.3
  7.8 0.1 reshape.56.pc_ref
  7.9 0.0 copy-done.4
  7.9 0.1 copy.26.ow_ref
  8.0 0.0 copy-done.1
  8.0 0.1 copy.23.w2_ref
  8.1 0.0 copy-done.2
  8.1 0.2 copy.19
  8.3 0.1 reshape.52
  8.4 0.0 copy-done
  8.5 0.1 copy.21
  8.6 0.1 copy.24.w3_ref
  8.8 0.1 copy.25.w3b_ref
  9.0 0.1 pad_maximum_fusion
  9.1 0.2 copy.20
  9.2 0.4 reshape.53.w1_ref
  9.7 0.1 fusion.17.w2b_ref
  9.8 0.2 select_convert_fusion.3.regroup_ref
  10.0 0.6 select_convert_fusion
  10.6 18.9 %all-to-all-done.x_ref = bf16[16,192,256]{2,1,0:T(8,128)(2,1)S(1)} async-done(((bf16[16,192,256]{2,1,0:T(8,128)(2,1)}), bf16[16,192,256]{2,1,0:T(8,128)(2,1)S(1)}, u32[]{:S(2)}, u32[]{:S(2)}) %all-to-all-start) | async-done | bytes 1572896 | tf_op jit(solution)/shard_map/all_to_all | solution.py:315
  29.5 6.2 %scenario.1 = (f32[16,128]{1,0:T(8,128)S(1)}, bf16[16,168,128]{2,1,0:T(8,128)(2,1)S(1)}) custom-call(bf16[16,192,256]{2,1,0:T(8,128)(2,1)S(1)} %all-to-all-done.x_ref, bf16[128,960]{1,0:T(8,128)(2,1)S(1)} %reshape.53.w1_ref, bf16[64,288]{1,0:T(8,128)(2,1)S(1)} %copy.23.w2_ref, bf16[64,576]{1,0:T(8,128)(2,1)S(1)} %copy.24.w3_ref, ...), custom_call_target="tpu_custom_call" | custom-call | flops 4000000000 | bytes 4194304 | tf_op jit(solution)/shard_map/scenario/pallas_call | solution.py:302
  35.7 16.7 %all_to_all.20.got_ref = bf16[16,168,128]{2,1,0:T(8,128)(2,1)S(1)} all-to-all(bf16[16,168,128]{2,1,0:T(8,128)(2,1)S(1)} %get-tuple-element.13), channel_id=1, replica_groups=mesh['lon'=16,'rep'=16] {'lon'}, dimensions={0} | all-to-all | bytes 1376256 | tf_op jit(solution)/shard_map/all_to_all | solution.py:315
  52.4 15.5 %all_to_all.21.got_ref = bf16[8,40,128]{2,1,0:T(8,128)(2,1)S(1)} all-to-all(bf16[8,40,128]{2,1,0:T(8,128)(2,1)S(1)} %lon_share.1), channel_id=1, replica_groups={{0,2,4,6,8,10,12,14},{1,3,5,7,9,11,13,15},{16,18,20,22,24,26,28,30},{17..., dimensions={0} | all-to-all | bytes 163840 | tf_op jit(solution)/shard_map/all_to_all | solution.py:315
  67.9 0.7 line_share.1
  68.7 6.6 %all-to-all-start.3 = ((bf16[32,40,128]{2,1,0:T(8,128)(2,1)}), bf16[32,40,128]{2,1,0:T(8,128)(2,1)S(1)}, u32[]{:S(2)}, u32[]{:S(2)}) async-start(bf16[32,40,128]{2,1,0:T(8,128)(2,1)} %line_share.1), calls=%async_computation.3 | async-start | bytes 655360 | tf_op jit(solution)/shard_map/all_to_all | solution.py:315
  75.3 0.1 reshape.57
  75.3 0.6 copy.27
  76.0 1.1 %copy.31 = bf16[16,4,32,128]{3,1,2,0:T(4,128)(2,1)} copy(bf16[16,4,32,128]{3,2,1,0:T(8,128)(2,1)S(1)} %bitcast.73) | data formatting | bytes 1048576 | tf_op jit(solution)/shard_map/reshape | solution.py:394
  77.1 7.8 %all-to-all-done.3 = bf16[32,40,128]{2,1,0:T(8,128)(2,1)S(1)} async-done(((bf16[32,40,128]{2,1,0:T(8,128)(2,1)}), bf16[32,40,128]{2,1,0:T(8,128)(2,1)S(1)}, u32[]{:S(2)}, u32[]{:S(2)}) %all-to-all-start.3) | async-done | bytes 327712 | tf_op jit(solution)/shard_map/all_to_all | solution.py:315
  84.9 0.9 %unpack.1 = (f32[24,4,4,32]{3,2,1,0:T(4,128)}, f32[3,3,32,64]{3,2,1,0:T(8,128)}, f32[3,3,64,64]{3,2,1,0:T(8,128)}, f32[1,64]{1,0:T(1,128)}) custom-call(bf16[1280,128]{1,0:T(8,128)(2,1)S(1)} %bitcast.72), custom_call_target="tpu_custom_call" | custom-call | tf_op jit(solution)/shard_map/unpack/pallas_call | solution.py:354
  (19 shorter events, 0.2 us)
Async XLA Ops:
  0.6 7.2 %copy-start.3 = (f32[1,32,64]{2,1,0:T(8,128)S(1)}, f32[1,32,64]{2,1,0:T(8,128)}, u32[]{:S(2)}) copy-start(f32[1,32,64]{2,1,0:T(8,128)} %param.11) | copy-start | bytes 24580
  0.6 7.3 %copy-start.4 = (f32[64]{0:T(128)S(1)}, f32[64]{0:T(128)}, u32[]{:S(2)}) copy-start(f32[64]{0:T(128)} %param.10) | copy-start | bytes 772
  0.7 7.4 %copy-start.1 = (bf16[64,32,3,3]{0,1,3,2:T(8,128)(2,1)S(1)}, bf16[64,32,3,3]{0,1,3,2:T(8,128)(2,1)}, u32[]{:S(2)}) copy-start(bf16[64,32,3,3]{0,1,3,2:T(8,128)(2,1)} %param.8) | copy-start | bytes 110596
  0.7 7.5 %copy-start.2 = (bf16[32,24,4,4]{0,3,2,1:T(4,128)(2,1)S(1)}, bf16[32,24,4,4]{0,3,2,1:T(4,128)(2,1)}, u32[]{:S(2)}) copy-start(bf16[32,24,4,4]{0,3,2,1:T(4,128)(2,1)} %param.7) | copy-start | bytes 73732
  0.7 7.8 %copy-start = (bf16[64,64,3,3]{1,0,3,2:T(8,128)(2,1)S(1)}, bf16[64,64,3,3]{1,0,3,2:T(8,128)(2,1)}, u32[]{:S(2)}) copy-start(bf16[64,64,3,3]{1,0,3,2:T(8,128)(2,1)} %param.9) | copy-start | bytes 221188
  0.7 28.9 %all-to-all-start = ((bf16[16,192,256]{2,1,0:T(8,128)(2,1)}), bf16[16,192,256]{2,1,0:T(8,128)(2,1)S(1)}, u32[]{:S(2)}, u32[]{:S(2)}) async-start(bf16[16,192,256]{2,1,0:T(8,128)(2,1)} %bitcast.74), calls=%async_computation | async-start | bytes 3145728 | tf_op jit(solution)/shard_map/all_to_all | solution.py:315
  68.7 16.3 %all-to-all-start.3 = ((bf16[32,40,128]{2,1,0:T(8,128)(2,1)}), bf16[32,40,128]{2,1,0:T(8,128)(2,1)S(1)}, u32[]{:S(2)}, u32[]{:S(2)}) async-start(bf16[32,40,128]{2,1,0:T(8,128)(2,1)} %line_share.1), calls=%async_computation.3 | async-start | bytes 655360 | tf_op jit(solution)/shard_map/all_to_all | solution.py:315
